TPU v7x, 512 devices: a whole 4x4x16 slice. The times are simulated.
512 devices in a mesh: section: 8 (over z_lo), space: 64 (over y, z_hi, x, core).
Axes of the slice: x: 4, y: 4, z: 16 (z_hi: 2, z_lo: 8; z = z_hi * 8 + z_lo), core: 2. Of those that a mesh axis runs over, the one named last changes fastest.
Arguments:
- acts: bfloat16 [8, 2, 8192, 1024], P('section', None, 'space'), may hold values from -6 to 6
- upstream: bfloat16 [2, 8192, 1024], P(None, 'space'), may hold values from -4 to 4
- weights: bfloat16 [8, 1024, 1024], P('section'), may hold values from -0.1875 to 0.1875
- neighbours: int32 [8192, 6], P('space'), may hold values from 0 to 8191, as said below
Outputs:
- input_grads: bfloat16 [8, 2, 8192, 1024], P('section', None, 'space')
- weight_grads: float32 [8, 1024, 1024], P('section', 'space')
Inputs may be any that keep to these rules, and one draw needn't show every extreme that they name: neighbours[i, k] is a node at most 32 positions from node i along the node order, taken cyclically over all 8192 nodes; the distance 32 is reached on both sides.
All inputs are finite; a program needn't handle non-finite values.
Results may differ from a plain program's by a relative error of at most 0.014.
Values may be sent and summed in bfloat16 or wider, within the bound.
No kernel may reach another device: no remote copies, remote signals or barrier semaphores. Data moves between devices by JAX's collectives and lax.ppermute only.
A program may use at most 64 MiB of HBM per device.

v0:
```python
import jax
import jax.numpy as jnp
from jax import lax
from jax.sharding import PartitionSpec as P

K = 6
HALO = 32


def extended_2(block, sides, width):
    for axis, dim in sides:
        count = lax.axis_size(axis)
        forward = [(i, i + 1) for i in range(count - 1)]
        forward.append((count - 1, 0))
        backward = [(target, source) for source, target in forward]
        low = lax.ppermute(
            lax.slice_in_dim(block, block.shape[dim] - width, None, axis=dim), axis, forward
        )
        high = lax.ppermute(lax.slice_in_dim(block, 0, width, axis=dim), axis, backward)
        block = jnp.concatenate([low, block, high], axis=dim)
    return block


def shifted(value, axis, steps):
    count = lax.axis_size(axis)
    first, last = (max(0, -steps), min(count, count - steps))
    return lax.ppermute(value, axis, [(source, source + steps) for source in range(first, last)])


def shards(acts, upstream, weights, neighbours):
    section_count = lax.axis_size("section")
    section_id = lax.axis_index("section")
    shard = lax.axis_index("space")
    rows = neighbours.shape[0]
    width = weights.shape[2]
    micro = upstream.shape[0]
    total_nodes = rows * lax.axis_size("space")
    local_ids = jnp.mod(neighbours - shard * rows + HALO, total_nodes)
    flat_ids = local_ids.reshape(-1)
    weight = weights[0]
    inputs = acts[0]

    def products(extended, h_field, g_field, keep):
        picked = jnp.take(extended, local_ids, axis=0).astype(jnp.float32)
        z_field = (h_field.astype(jnp.float32) + jnp.mean(picked, axis=1)).astype(jnp.bfloat16)
        u_field = jnp.dot(z_field, weight, preferred_element_type=jnp.float32)
        sig = jax.nn.sigmoid(u_field)
        du_field = (g_field.astype(jnp.float32) * sig * (1.0 + u_field * (1.0 - sig))).astype(
            jnp.bfloat16
        )
        dz_field = lax.dot_general(
            du_field, weight, (((1,), (1,)), ((), ())), preferred_element_type=jnp.float32
        )
        keep = keep + lax.dot_general(
            z_field, du_field, (((0,), (0,)), ((), ())), preferred_element_type=jnp.float32
        )
        return (dz_field, keep)

    def tick(step, carry):
        received, grads, keep = carry
        batch = step - (section_count - 1 - section_id)
        valid = jnp.logical_and(batch >= 0, batch < micro)
        index = jnp.clip(batch, 0, micro - 1)
        h_field = lax.dynamic_index_in_dim(inputs, index, 0, False)
        g_field = jnp.where(
            section_id == section_count - 1,
            lax.dynamic_index_in_dim(upstream, index, 0, False),
            received,
        )
        extended = extended_2(h_field, (("space", 0),), HALO)

        def active(state):
            return products(extended, h_field, g_field, state)

        def resting(state):
            return (jnp.zeros((rows, width), jnp.float32), state)

        dz_field, keep = lax.cond(valid, active, resting, keep)
        share = dz_field * (1.0 / K)
        spread = (
            jnp.zeros((rows + 2 * HALO, width), jnp.float32)
            .at[flat_ids]
            .add(jnp.broadcast_to(share[:, None, :], (rows, K, width)).reshape(-1, width))
        )
        outgoing = jnp.concatenate([spread[:HALO], spread[rows + HALO :]], axis=0)
        returned = extended_2(outgoing.astype(jnp.bfloat16), (("space", 0),), HALO).astype(
            outgoing.dtype
        )
        own = spread[HALO : HALO + rows]
        own = own + jnp.pad(returned[:HALO], ((0, rows - HALO), (0, 0)))
        own = own + jnp.pad(returned[3 * HALO :], ((rows - HALO, 0), (0, 0)))
        d_input = (g_field.astype(jnp.float32) + dz_field + own).astype(jnp.bfloat16)
        updated = lax.dynamic_update_index_in_dim(grads, d_input, index, 0)
        grads = jnp.where(valid, updated, grads)
        received = shifted(d_input, "section", -1)
        return (received, grads, keep)

    keep_start = jnp.zeros((width, width), jnp.float32)
    start = (
        jnp.zeros((rows, width), jnp.bfloat16),
        jnp.zeros((micro, rows, width), jnp.bfloat16),
        keep_start,
    )
    received, grads, keep = lax.fori_loop(0, micro + section_count - 1, tick, start)
    weight_grad = lax.psum_scatter(keep, "space", scatter_dimension=0, tiled=True)
    return (grads[None], weight_grad[None])


def solution(mesh):
    in_specs = (
        P("section", None, "space", None),
        P(None, "space", None),
        P("section", None, None),
        P("space", None),
    )
    out_specs = (P("section", None, "space", None), P("section", "space", None))
    return jax.shard_map(shards, mesh=mesh, in_specs=in_specs, out_specs=out_specs, check_vma=False)
```

profile of v0, /device:TPU:32, one launch (start us, length us, event | category | flops | bytes accessed | tf_op | source)
XLA Modules:
  0.0 1351.0 jit_solution(14041849353182451122)
XLA Ops:
  11.6 763.5 %while.22 = (s32[]{:T(128)}, bf16[128,1024]{1,0:T(8,128)(2,1)S(1)}, bf16[2,128,1024]{2,1,0:T(8,128)(2,1)}, f32[1024,1024]{1,0:T(8,128)}, pred[]{:T(512)}, /*inde...) while((s32[]{:T(128)}, bf16[128,1024]{1,0:T(8,128)(2,1)S(1)}, ...), condition=%wide.region_5.6_spmd, body=%wide.region_0.5_spmd.sunk | while | flops 817833984 | bytes 88377048 | solution.py:104
  12.5 18.9 %collective-permute-start = (bf16[32,1024]{1,0:T(8,128)(2,1)S(1)}, bf16[32,1024]{1,0:T(8,128)(2,1)S(1)}, u32[]{:S(2)}, u32[]{:S(2)}) collective-permute-start(bf16[32,1024]{1,0:T(8,128)(2,1)S(1)} %get-tuple-element.394), channel_id=1, source_target_pairs={{1,0},{2,1},{3,2},{4,3},{5,4},{6,5},{7,6},{8,7},{9,8},{10,9},{11,1... | collective-permute-start | bytes 196616 | tf_op jit(solution)/shard_map/while/body/eval_jaxpr/ppermute | solution.py:19
  35.3 14.6 %collective-permute-done.1 = bf16[32,1024]{1,0:T(8,128)(2,1)S(1)} collective-permute-done((bf16[32,1024]{1,0:T(8,128)(2,1)S(1)}, bf16[32,1024]{1,0:T(8,128)(2,1)S(1)}, u32[]{:S(2)}, u32[]{:S(2)}) %collective-permute-start.1) | collective-permute-done | bytes 65568 | tf_op jit(solution)/shard_map/while/body/eval_jaxpr/ppermute | solution.py:16
  72.2 16.3 %collective-permute-done.3 = bf16[32,1024]{1,0:T(8,128)(2,1)S(1)} collective-permute-done((bf16[32,1024]{1,0:T(8,128)(2,1)S(1)}, bf16[32,1024]{1,0:T(8,128)(2,1)S(1)}, u32[]{:S(2)}, u32[]{:S(2)}) %collective-permute-start.3) | collective-permute-done | bytes 65568 | tf_op jit(solution)/shard_map/while/body/eval_jaxpr/ppermute | solution.py:16
  106.6 14.1 %collective-permute-done.1 = bf16[32,1024]{1,0:T(8,128)(2,1)S(1)} collective-permute-done((bf16[32,1024]{1,0:T(8,128)(2,1)S(1)}, bf16[32,1024]{1,0:T(8,128)(2,1)S(1)}, u32[]{:S(2)}, u32[]{:S(2)}) %collective-permute-start.1) | collective-permute-done | bytes 65568 | tf_op jit(solution)/shard_map/while/body/eval_jaxpr/ppermute | solution.py:16
  143.0 16.2 %collective-permute-done.3 = bf16[32,1024]{1,0:T(8,128)(2,1)S(1)} collective-permute-done((bf16[32,1024]{1,0:T(8,128)(2,1)S(1)}, bf16[32,1024]{1,0:T(8,128)(2,1)S(1)}, u32[]{:S(2)}, u32[]{:S(2)}) %collective-permute-start.3) | collective-permute-done | bytes 65568 | tf_op jit(solution)/shard_map/while/body/eval_jaxpr/ppermute | solution.py:16
  177.3 14.1 %collective-permute-done.1 = bf16[32,1024]{1,0:T(8,128)(2,1)S(1)} collective-permute-done((bf16[32,1024]{1,0:T(8,128)(2,1)S(1)}, bf16[32,1024]{1,0:T(8,128)(2,1)S(1)}, u32[]{:S(2)}, u32[]{:S(2)}) %collective-permute-start.1) | collective-permute-done | bytes 65568 | tf_op jit(solution)/shard_map/while/body/eval_jaxpr/ppermute | solution.py:16
  213.7 16.2 %collective-permute-done.3 = bf16[32,1024]{1,0:T(8,128)(2,1)S(1)} collective-permute-done((bf16[32,1024]{1,0:T(8,128)(2,1)S(1)}, bf16[32,1024]{1,0:T(8,128)(2,1)S(1)}, u32[]{:S(2)}, u32[]{:S(2)}) %collective-permute-start.3) | collective-permute-done | bytes 65568 | tf_op jit(solution)/shard_map/while/body/eval_jaxpr/ppermute | solution.py:16
  248.0 14.2 %collective-permute-done.1 = bf16[32,1024]{1,0:T(8,128)(2,1)S(1)} collective-permute-done((bf16[32,1024]{1,0:T(8,128)(2,1)S(1)}, bf16[32,1024]{1,0:T(8,128)(2,1)S(1)}, u32[]{:S(2)}, u32[]{:S(2)}) %collective-permute-start.1) | collective-permute-done | bytes 65568 | tf_op jit(solution)/shard_map/while/body/eval_jaxpr/ppermute | solution.py:16
  285.3 16.7 %collective-permute-done.3 = bf16[32,1024]{1,0:T(8,128)(2,1)S(1)} collective-permute-done((bf16[32,1024]{1,0:T(8,128)(2,1)S(1)}, bf16[32,1024]{1,0:T(8,128)(2,1)S(1)}, u32[]{:S(2)}, u32[]{:S(2)}) %collective-permute-start.3) | collective-permute-done | bytes 65568 | tf_op jit(solution)/shard_map/while/body/eval_jaxpr/ppermute | solution.py:16
  319.4 14.1 %collective-permute-done.1 = bf16[32,1024]{1,0:T(8,128)(2,1)S(1)} collective-permute-done((bf16[32,1024]{1,0:T(8,128)(2,1)S(1)}, bf16[32,1024]{1,0:T(8,128)(2,1)S(1)}, u32[]{:S(2)}, u32[]{:S(2)}) %collective-permute-start.1) | collective-permute-done | bytes 65568 | tf_op jit(solution)/shard_map/while/body/eval_jaxpr/ppermute | solution.py:16
  355.8 16.2 %collective-permute-done.3 = bf16[32,1024]{1,0:T(8,128)(2,1)S(1)} collective-permute-done((bf16[32,1024]{1,0:T(8,128)(2,1)S(1)}, bf16[32,1024]{1,0:T(8,128)(2,1)S(1)}, u32[]{:S(2)}, u32[]{:S(2)}) %collective-permute-start.3) | collective-permute-done | bytes 65568 | tf_op jit(solution)/shard_map/while/body/eval_jaxpr/ppermute | solution.py:16
  389.4 14.2 %collective-permute-done.1 = bf16[32,1024]{1,0:T(8,128)(2,1)S(1)} collective-permute-done((bf16[32,1024]{1,0:T(8,128)(2,1)S(1)}, bf16[32,1024]{1,0:T(8,128)(2,1)S(1)}, u32[]{:S(2)}, u32[]{:S(2)}) %collective-permute-start.1) | collective-permute-done | bytes 65568 | tf_op jit(solution)/shard_map/while/body/eval_jaxpr/ppermute | solution.py:16
  425.9 16.2 %collective-permute-done.3 = bf16[32,1024]{1,0:T(8,128)(2,1)S(1)} collective-permute-done((bf16[32,1024]{1,0:T(8,128)(2,1)S(1)}, bf16[32,1024]{1,0:T(8,128)(2,1)S(1)}, u32[]{:S(2)}, u32[]{:S(2)}) %collective-permute-start.3) | collective-permute-done | bytes 65568 | tf_op jit(solution)/shard_map/while/body/eval_jaxpr/ppermute | solution.py:16
  446.0 78.5 %collective-permute-done.4 = bf16[128,1024]{1,0:T(8,128)(2,1)S(1)} collective-permute-done((bf16[128,1024]{1,0:T(8,128)(2,1)S(1)}, bf16[128,1024]{1,0:T(8,128)(2,1)S(1)}, u32[]{:S(2)}, u32[]{:S(2)}) %collective-permute-start.4) | collective-permute-done | bytes 262176 | tf_op jit(solution)/shard_map/while/body/eval_jaxpr/ppermute | solution.py:27
  531.8 14.1 %collective-permute-done.1 = bf16[32,1024]{1,0:T(8,128)(2,1)S(1)} collective-permute-done((bf16[32,1024]{1,0:T(8,128)(2,1)S(1)}, bf16[32,1024]{1,0:T(8,128)(2,1)S(1)}, u32[]{:S(2)}, u32[]{:S(2)}) %collective-permute-start.1) | collective-permute-done | bytes 65568 | tf_op jit(solution)/shard_map/while/body/eval_jaxpr/ppermute | solution.py:16
  545.9 13.6 %conditional.2 = (f32[128,1024]{1,0:T(8,128)S(1)}, f32[1024,1024]{1,0:T(8,128)}) conditional(s32[]{:T(128)} %convert_element_type.97, f32[1024,1024]{1,0:T(8,128)} %get-tuple-element.426, (bf16[128,1024]{1,0:T(8,128)(2,1)S(1)}, bf16[128,1024]{1,0:T(8,128)(2,1)S(1)}, s32[128,6]{1,0:T(8,128)S(1)}, bf16[192,1024]{1,0:T(8,128)(2,1)S(1)}, ...), branch_computations={%region_1.1_spmd, %region_2.3_spmd} | conditional | flops 812261120 | bytes 67136096 | solution.py:78
  581.7 16.2 %collective-permute-done.3 = bf16[32,1024]{1,0:T(8,128)(2,1)S(1)} collective-permute-done((bf16[32,1024]{1,0:T(8,128)(2,1)S(1)}, bf16[32,1024]{1,0:T(8,128)(2,1)S(1)}, u32[]{:S(2)}, u32[]{:S(2)}) %collective-permute-start.3) | collective-permute-done | bytes 65568 | tf_op jit(solution)/shard_map/while/body/eval_jaxpr/ppermute | solution.py:16
  616.8 15.1 %collective-permute-done.1 = bf16[32,1024]{1,0:T(8,128)(2,1)S(1)} collective-permute-done((bf16[32,1024]{1,0:T(8,128)(2,1)S(1)}, bf16[32,1024]{1,0:T(8,128)(2,1)S(1)}, u32[]{:S(2)}, u32[]{:S(2)}) %collective-permute-start.1) | collective-permute-done | bytes 65568 | tf_op jit(solution)/shard_map/while/body/eval_jaxpr/ppermute | solution.py:16
  667.7 16.2 %collective-permute-done.3 = bf16[32,1024]{1,0:T(8,128)(2,1)S(1)} collective-permute-done((bf16[32,1024]{1,0:T(8,128)(2,1)S(1)}, bf16[32,1024]{1,0:T(8,128)(2,1)S(1)}, u32[]{:S(2)}, u32[]{:S(2)}) %collective-permute-start.3) | collective-permute-done | bytes 65568 | tf_op jit(solution)/shard_map/while/body/eval_jaxpr/ppermute | solution.py:16
  701.3 14.1 %collective-permute-done.1 = bf16[32,1024]{1,0:T(8,128)(2,1)S(1)} collective-permute-done((bf16[32,1024]{1,0:T(8,128)(2,1)S(1)}, bf16[32,1024]{1,0:T(8,128)(2,1)S(1)}, u32[]{:S(2)}, u32[]{:S(2)}) %collective-permute-start.1) | collective-permute-done | bytes 65568 | tf_op jit(solution)/shard_map/while/body/eval_jaxpr/ppermute | solution.py:16
  737.7 16.2 %collective-permute-done.3 = bf16[32,1024]{1,0:T(8,128)(2,1)S(1)} collective-permute-done((bf16[32,1024]{1,0:T(8,128)(2,1)S(1)}, bf16[32,1024]{1,0:T(8,128)(2,1)S(1)}, u32[]{:S(2)}, u32[]{:S(2)}) %collective-permute-start.3) | collective-permute-done | bytes 65568 | tf_op jit(solution)/shard_map/while/body/eval_jaxpr/ppermute | solution.py:16
  755.8 15.4 %collective-permute-start.4 = (bf16[128,1024]{1,0:T(8,128)(2,1)S(1)}, bf16[128,1024]{1,0:T(8,128)(2,1)S(1)}, u32[]{:S(2)}, u32[]{:S(2)}) collective-permute-start(bf16[128,1024]{1,0:T(8,128)(2,1)S(1)} %get-tuple-element.399), channel_id=1, source_target_pairs={{64,0},{128,64},{192,128},{256,192},{320,256},{384,320},{448,384},... | collective-permute-start | bytes 786440 | tf_op jit(solution)/shard_map/while/body/eval_jaxpr/ppermute | solution.py:27
  775.1 569.0 %reduce-scatter.2.cloned.1.call-done = f32[16,1024]{1,0:T(8,128)} async-done(((f32[1024,1024]{1,0:T(8,128)}), f32[16,1024]{1,0:T(8,128)}) %reduce-scatter.2.cloned.1.call-update) | async-done | bytes 65552 | tf_op jit(solution)/shard_map/reduce_scatter | solution.py:105
  (252 shorter events, 392.6 us)
Async XLA Ops:
  7.2 1337.0 %reduce-scatter.2.cloned.1.call-start = ((), (), s32[]{:S(2)}) async-start(), calls=%async_computation.1 | async-start | bytes 4259840 | tf_op jit(solution)/shard_map/reduce_scatter | solution.py:105
  12.5 22.8 %collective-permute-start = (bf16[32,1024]{1,0:T(8,128)(2,1)S(1)}, bf16[32,1024]{1,0:T(8,128)(2,1)S(1)}, u32[]{:S(2)}, u32[]{:S(2)}) collective-permute-start(bf16[32,1024]{1,0:T(8,128)(2,1)S(1)} %get-tuple-element.394), channel_id=1, source_target_pairs={{1,0},{2,1},{3,2},{4,3},{5,4},{6,5},{7,6},{8,7},{9,8},{10,9},{11,1... | collective-permute-start | bytes 196616 | tf_op jit(solution)/shard_map/while/body/eval_jaxpr/ppermute | solution.py:19
  31.4 18.5 %collective-permute-start.1 = (bf16[32,1024]{1,0:T(8,128)(2,1)S(1)}, bf16[32,1024]{1,0:T(8,128)(2,1)S(1)}, u32[]{:S(2)}, u32[]{:S(2)}) collective-permute-start(bf16[32,1024]{1,0:T(8,128)(2,1)S(1)} %get-tuple-element.395), channel_id=1, source_target_pairs={{0,1},{1,2},{2,3},{3,4},{4,5},{5,6},{6,7},{7,8},{8,9},{9,10},{10,1... | collective-permute-start | bytes 196616 | tf_op jit(solution)/shard_map/while/body/eval_jaxpr/ppermute | solution.py:16
  69.9 18.6 %collective-permute-start.3 = (bf16[32,1024]{1,0:T(8,128)(2,1)S(1)}, bf16[32,1024]{1,0:T(8,128)(2,1)S(1)}, u32[]{:S(2)}, u32[]{:S(2)}) collective-permute-start(bf16[32,1024]{1,0:T(8,128)(2,1)S(1)} %get-tuple-element.398), channel_id=1, source_target_pairs={{0,1},{1,2},{2,3},{3,4},{4,5},{5,6},{6,7},{7,8},{8,9},{9,10},{10,1... | collective-permute-start | bytes 196616 | tf_op jit(solution)/shard_map/while/body/eval_jaxpr/ppermute | solution.py:16
  90.4 9.0 collective-permute-start.4
  102.2 18.5 %collective-permute-start.1 = (bf16[32,1024]{1,0:T(8,128)(2,1)S(1)}, bf16[32,1024]{1,0:T(8,128)(2,1)S(1)}, u32[]{:S(2)}, u32[]{:S(2)}) collective-permute-start(bf16[32,1024]{1,0:T(8,128)(2,1)S(1)} %get-tuple-element.395), channel_id=1, source_target_pairs={{0,1},{1,2},{2,3},{3,4},{4,5},{5,6},{6,7},{7,8},{8,9},{9,10},{10,1... | collective-permute-start | bytes 196616 | tf_op jit(solution)/shard_map/while/body/eval_jaxpr/ppermute | solution.py:16
  140.7 18.5 %collective-permute-start.3 = (bf16[32,1024]{1,0:T(8,128)(2,1)S(1)}, bf16[32,1024]{1,0:T(8,128)(2,1)S(1)}, u32[]{:S(2)}, u32[]{:S(2)}) collective-permute-start(bf16[32,1024]{1,0:T(8,128)(2,1)S(1)} %get-tuple-element.398), channel_id=1, source_target_pairs={{0,1},{1,2},{2,3},{3,4},{4,5},{5,6},{6,7},{7,8},{8,9},{9,10},{10,1... | collective-permute-start | bytes 196616 | tf_op jit(solution)/shard_map/while/body/eval_jaxpr/ppermute | solution.py:16
  172.9 18.5 %collective-permute-start.1 = (bf16[32,1024]{1,0:T(8,128)(2,1)S(1)}, bf16[32,1024]{1,0:T(8,128)(2,1)S(1)}, u32[]{:S(2)}, u32[]{:S(2)}) collective-permute-start(bf16[32,1024]{1,0:T(8,128)(2,1)S(1)} %get-tuple-element.395), channel_id=1, source_target_pairs={{0,1},{1,2},{2,3},{3,4},{4,5},{5,6},{6,7},{7,8},{8,9},{9,10},{10,1... | collective-permute-start | bytes 196616 | tf_op jit(solution)/shard_map/while/body/eval_jaxpr/ppermute | solution.py:16
  211.4 18.5 %collective-permute-start.3 = (bf16[32,1024]{1,0:T(8,128)(2,1)S(1)}, bf16[32,1024]{1,0:T(8,128)(2,1)S(1)}, u32[]{:S(2)}, u32[]{:S(2)}) collective-permute-start(bf16[32,1024]{1,0:T(8,128)(2,1)S(1)} %get-tuple-element.398), channel_id=1, source_target_pairs={{0,1},{1,2},{2,3},{3,4},{4,5},{5,6},{6,7},{7,8},{8,9},{9,10},{10,1... | collective-permute-start | bytes 196616 | tf_op jit(solution)/shard_map/while/body/eval_jaxpr/ppermute | solution.py:16
  243.6 18.6 %collective-permute-start.1 = (bf16[32,1024]{1,0:T(8,128)(2,1)S(1)}, bf16[32,1024]{1,0:T(8,128)(2,1)S(1)}, u32[]{:S(2)}, u32[]{:S(2)}) collective-permute-start(bf16[32,1024]{1,0:T(8,128)(2,1)S(1)} %get-tuple-element.395), channel_id=1, source_target_pairs={{0,1},{1,2},{2,3},{3,4},{4,5},{5,6},{6,7},{7,8},{8,9},{9,10},{10,1... | collective-permute-start | bytes 196616 | tf_op jit(solution)/shard_map/while/body/eval_jaxpr/ppermute | solution.py:16
  282.1 19.9 %collective-permute-start.3 = (bf16[32,1024]{1,0:T(8,128)(2,1)S(1)}, bf16[32,1024]{1,0:T(8,128)(2,1)S(1)}, u32[]{:S(2)}, u32[]{:S(2)}) collective-permute-start(bf16[32,1024]{1,0:T(8,128)(2,1)S(1)} %get-tuple-element.398), channel_id=1, source_target_pairs={{0,1},{1,2},{2,3},{3,4},{4,5},{5,6},{6,7},{7,8},{8,9},{9,10},{10,1... | collective-permute-start | bytes 196616 | tf_op jit(solution)/shard_map/while/body/eval_jaxpr/ppermute | solution.py:16
  315.0 18.5 %collective-permute-start.1 = (bf16[32,1024]{1,0:T(8,128)(2,1)S(1)}, bf16[32,1024]{1,0:T(8,128)(2,1)S(1)}, u32[]{:S(2)}, u32[]{:S(2)}) collective-permute-start(bf16[32,1024]{1,0:T(8,128)(2,1)S(1)} %get-tuple-element.395), channel_id=1, source_target_pairs={{0,1},{1,2},{2,3},{3,4},{4,5},{5,6},{6,7},{7,8},{8,9},{9,10},{10,1... | collective-permute-start | bytes 196616 | tf_op jit(solution)/shard_map/while/body/eval_jaxpr/ppermute | solution.py:16
  353.5 18.5 %collective-permute-start.3 = (bf16[32,1024]{1,0:T(8,128)(2,1)S(1)}, bf16[32,1024]{1,0:T(8,128)(2,1)S(1)}, u32[]{:S(2)}, u32[]{:S(2)}) collective-permute-start(bf16[32,1024]{1,0:T(8,128)(2,1)S(1)} %get-tuple-element.398), channel_id=1, source_target_pairs={{0,1},{1,2},{2,3},{3,4},{4,5},{5,6},{6,7},{7,8},{8,9},{9,10},{10,1... | collective-permute-start | bytes 196616 | tf_op jit(solution)/shard_map/while/body/eval_jaxpr/ppermute | solution.py:16
  385.0 18.6 %collective-permute-start.1 = (bf16[32,1024]{1,0:T(8,128)(2,1)S(1)}, bf16[32,1024]{1,0:T(8,128)(2,1)S(1)}, u32[]{:S(2)}, u32[]{:S(2)}) collective-permute-start(bf16[32,1024]{1,0:T(8,128)(2,1)S(1)} %get-tuple-element.395), channel_id=1, source_target_pairs={{0,1},{1,2},{2,3},{3,4},{4,5},{5,6},{6,7},{7,8},{8,9},{9,10},{10,1... | collective-permute-start | bytes 196616 | tf_op jit(solution)/shard_map/while/body/eval_jaxpr/ppermute | solution.py:16
  423.5 18.6 %collective-permute-start.3 = (bf16[32,1024]{1,0:T(8,128)(2,1)S(1)}, bf16[32,1024]{1,0:T(8,128)(2,1)S(1)}, u32[]{:S(2)}, u32[]{:S(2)}) collective-permute-start(bf16[32,1024]{1,0:T(8,128)(2,1)S(1)} %get-tuple-element.398), channel_id=1, source_target_pairs={{0,1},{1,2},{2,3},{3,4},{4,5},{5,6},{6,7},{7,8},{8,9},{9,10},{10,1... | collective-permute-start | bytes 196616 | tf_op jit(solution)/shard_map/while/body/eval_jaxpr/ppermute | solution.py:16
  444.1 80.5 %collective-permute-start.4 = (bf16[128,1024]{1,0:T(8,128)(2,1)S(1)}, bf16[128,1024]{1,0:T(8,128)(2,1)S(1)}, u32[]{:S(2)}, u32[]{:S(2)}) collective-permute-start(bf16[128,1024]{1,0:T(8,128)(2,1)S(1)} %get-tuple-element.399), channel_id=1, source_target_pairs={{64,0},{128,64},{192,128},{256,192},{320,256},{384,320},{448,384},... | collective-permute-start | bytes 786440 | tf_op jit(solution)/shard_map/while/body/eval_jaxpr/ppermute | solution.py:27
  527.3 18.5 %collective-permute-start.1 = (bf16[32,1024]{1,0:T(8,128)(2,1)S(1)}, bf16[32,1024]{1,0:T(8,128)(2,1)S(1)}, u32[]{:S(2)}, u32[]{:S(2)}) collective-permute-start(bf16[32,1024]{1,0:T(8,128)(2,1)S(1)} %get-tuple-element.395), channel_id=1, source_target_pairs={{0,1},{1,2},{2,3},{3,4},{4,5},{5,6},{6,7},{7,8},{8,9},{9,10},{10,1... | collective-permute-start | bytes 196616 | tf_op jit(solution)/shard_map/while/body/eval_jaxpr/ppermute | solution.py:16
  579.3 18.5 %collective-permute-start.3 = (bf16[32,1024]{1,0:T(8,128)(2,1)S(1)}, bf16[32,1024]{1,0:T(8,128)(2,1)S(1)}, u32[]{:S(2)}, u32[]{:S(2)}) collective-permute-start(bf16[32,1024]{1,0:T(8,128)(2,1)S(1)} %get-tuple-element.398), channel_id=1, source_target_pairs={{0,1},{1,2},{2,3},{3,4},{4,5},{5,6},{6,7},{7,8},{8,9},{9,10},{10,1... | collective-permute-start | bytes 196616 | tf_op jit(solution)/shard_map/while/body/eval_jaxpr/ppermute | solution.py:16
  599.8 9.7 collective-permute-start.4
  612.3 19.5 %collective-permute-start.1 = (bf16[32,1024]{1,0:T(8,128)(2,1)S(1)}, bf16[32,1024]{1,0:T(8,128)(2,1)S(1)}, u32[]{:S(2)}, u32[]{:S(2)}) collective-permute-start(bf16[32,1024]{1,0:T(8,128)(2,1)S(1)} %get-tuple-element.395), channel_id=1, source_target_pairs={{0,1},{1,2},{2,3},{3,4},{4,5},{5,6},{6,7},{7,8},{8,9},{9,10},{10,1... | collective-permute-start | bytes 196616 | tf_op jit(solution)/shard_map/while/body/eval_jaxpr/ppermute | solution.py:16
  665.2 18.6 %collective-permute-start.3 = (bf16[32,1024]{1,0:T(8,128)(2,1)S(1)}, bf16[32,1024]{1,0:T(8,128)(2,1)S(1)}, u32[]{:S(2)}, u32[]{:S(2)}) collective-permute-start(bf16[32,1024]{1,0:T(8,128)(2,1)S(1)} %get-tuple-element.398), channel_id=1, source_target_pairs={{0,1},{1,2},{2,3},{3,4},{4,5},{5,6},{6,7},{7,8},{8,9},{9,10},{10,1... | collective-permute-start | bytes 196616 | tf_op jit(solution)/shard_map/while/body/eval_jaxpr/ppermute | solution.py:16
  696.9 18.5 %collective-permute-start.1 = (bf16[32,1024]{1,0:T(8,128)(2,1)S(1)}, bf16[32,1024]{1,0:T(8,128)(2,1)S(1)}, u32[]{:S(2)}, u32[]{:S(2)}) collective-permute-start(bf16[32,1024]{1,0:T(8,128)(2,1)S(1)} %get-tuple-element.395), channel_id=1, source_target_pairs={{0,1},{1,2},{2,3},{3,4},{4,5},{5,6},{6,7},{7,8},{8,9},{9,10},{10,1... | collective-permute-start | bytes 196616 | tf_op jit(solution)/shard_map/while/body/eval_jaxpr/ppermute | solution.py:16
  735.4 18.5 %collective-permute-start.3 = (bf16[32,1024]{1,0:T(8,128)(2,1)S(1)}, bf16[32,1024]{1,0:T(8,128)(2,1)S(1)}, u32[]{:S(2)}, u32[]{:S(2)}) collective-permute-start(bf16[32,1024]{1,0:T(8,128)(2,1)S(1)} %get-tuple-element.398), channel_id=1, source_target_pairs={{0,1},{1,2},{2,3},{3,4},{4,5},{5,6},{6,7},{7,8},{8,9},{9,10},{10,1... | collective-permute-start | bytes 196616 | tf_op jit(solution)/shard_map/while/body/eval_jaxpr/ppermute | solution.py:16
  755.8 19.3 %collective-permute-start.4 = (bf16[128,1024]{1,0:T(8,128)(2,1)S(1)}, bf16[128,1024]{1,0:T(8,128)(2,1)S(1)}, u32[]{:S(2)}, u32[]{:S(2)}) collective-permute-start(bf16[128,1024]{1,0:T(8,128)(2,1)S(1)} %get-tuple-element.399), channel_id=1, source_target_pairs={{64,0},{128,64},{192,128},{256,192},{320,256},{384,320},{448,384},... | collective-permute-start | bytes 786440 | tf_op jit(solution)/shard_map/while/body/eval_jaxpr/ppermute | solution.py:27
  (29 other events, 155.6 us)
Sparse Core Ops, SparseCore 0:
  775.3 568.8 reduce-scatter.1
where the time goes:
time: 1350 us
  waiting for transfers between devices  974 us (72%)
  other arithmetic  129 us (10%)
  starting transfers between devices  126 us (9%)
  local copies, waits for them, and re-layouts  96.9 us (7%)
  between operations  14.1 us (1%)
    reduce_scatter x1, waiting for transfers between devices, shards(): lax.psum_scatter(keep, 'space', scatter_dimension=0, tiled=True)  569 us
    ppermute x18, waiting for transfers between devices, extended_2(): lax.ppermute(lax.slice_in_dim(block, block.shape[dim] - width, None, axis...  275 us
    ppermute x9, waiting for transfers between devices, shifted(): lax.ppermute(value, axis, [(source, source + steps) for source in range(f...  129 us
    scatter-add x9, other arithmetic, tick(): spread = jnp.zeros((rows + 2 * HALO, width), jnp.float32).at[flat_ids].ad...  94.5 us
    ppermute x18, starting transfers between devices, extended_2(): lax.ppermute(lax.slice_in_dim(block, 0, width, axis=dim), axis, backward)  52.1 us
    reshape x9, local copies, waits for them, and re-layouts, tick(): jnp.broadcast_to(share[:, None, :], (rows, K, width)).reshape(-1, width)  42.5 us
    ppermute x18, starting transfers between devices, extended_2(): lax.ppermute(lax.slice_in_dim(block, block.shape[dim] - width, None, axis...  42.3 us
    ppermute x9, starting transfers between devices, shifted(): lax.ppermute(value, axis, [(source, source + steps) for source in range(f...  31.8 us
  transfers between devices with their start and end apart: 46, of which 29 were waited for; matrix products, arithmetic and copies ran while one was open for 1% of the time, Pallas kernels for 0%

commit v1 on v0

v1 whole, which is shorter than its diff:
```python
import functools

import jax
import jax.numpy as jnp
from jax import lax
from jax.experimental import pallas as pl
from jax.experimental.pallas import tpu as pltpu
from jax.sharding import PartitionSpec as P


K = 6
HALO = 32
EDGE = 2 * HALO
AXES = ("section", "space")

bf16 = jnp.bfloat16
f32 = jnp.float32
VMEM = pl.BlockSpec(memory_space=pltpu.VMEM)
SMEM = pl.BlockSpec(memory_space=pltpu.SMEM)
LIMIT = pltpu.CompilerParams(vmem_limit_bytes=16 * 1024 * 1024)
EVEN, NEAR, FAR, LOWER, BASE, NODES = 8, 9, 10, 11, 12, 13


def on_chip(value):
    return pltpu.with_memory_space_constraint(value, pltpu.VMEM)


def permute(value, pairs):
    return lax.ppermute(value, AXES, pairs)


def call(kernel, outs, flags, arrays, aliases=None):
    return pl.pallas_call(
        kernel,
        out_shape=tuple(pltpu.VMEM(shape, dtype) for shape, dtype in outs),
        in_specs=[SMEM] + [VMEM] * len(arrays),
        out_specs=tuple([VMEM] * len(outs)),
        input_output_aliases=aliases or {},
        compiler_params=LIMIT,
    )(flags, *[on_chip(a) for a in arrays])


def turn_kernel(flags, w, out):
    out[...] = w[...].T


def pack_kernel(flags, h, up, neighbours, off, *edges):
    micro, rows, width = h.shape
    nodes = flags[NODES]
    even = flags[EVEN] == 1
    ids = flags[BASE] + lax.broadcasted_iota(jnp.int32, neighbours.shape, 0)
    step = neighbours[...] - ids
    step = jnp.where(step > HALO, step - nodes, step)
    step = jnp.where(step < -HALO, step + nodes, step)
    off[...] = jnp.zeros(off.shape, bf16)
    off[:, :K] = step.astype(f32).astype(bf16)
    blank = jnp.zeros((16, width - 256), bf16)

    def edge(upper):
        def cut(value, size):
            return value[rows - size :] if upper else value[:size]

        steps = cut(off, HALO)
        steps = jnp.concatenate([steps[:16], steps[16:], blank], axis=1)
        inner = [cut(h[m], EDGE) for m in range(micro)] + [steps]
        return jnp.concatenate(inner + [cut(up[m], HALO) for m in range(micro)], axis=0)

    lower, upper = edge(False), edge(True)
    x, y = jnp.where(even, upper, lower), jnp.where(even, lower, upper)
    for value, full, short in ((x, edges[0], edges[2]), (y, edges[1], edges[3])):
        full[...] = value
        short[...] = value[: short.shape[0]]


def prepare_kernel(active, flags, h, off, w, from_x, from_y, *refs):
    factor, mix, z_out = refs[-3:]
    micro, rows, _ = h.shape
    span = rows + 2 * HALO
    reach = rows + 2 * EDGE

    @pl.when(flags[active] == 1)
    def _():
        even = flags[EVEN] == 1

        def both(start, size):
            x, y = from_x[start : start + size, :], from_y[start : start + size, :]
            return jnp.where(even, y, x), jnp.where(even, x, y)

        low, high = both(micro * EDGE, 16)
        steps = jnp.concatenate(
            [low[:, :128], low[:, 128:256], off[...], high[:, :128], high[:, 128:256]], axis=0
        ).astype(f32)
        column = lax.broadcasted_iota(jnp.int32, (span, reach), 1).astype(f32)
        row = lax.broadcasted_iota(jnp.int32, (span, reach), 0).astype(f32)
        distance = column - row - float(HALO)
        count = jnp.zeros((span, reach), f32)
        for k in range(K):
            count = count + jnp.where(distance == steps[:, k : k + 1], 1.0, 0.0)
        gather = count.astype(bf16)
        spread = (count + jnp.where(distance == 0.0, float(K), 0.0)).T
        mix[...] = spread[EDGE : EDGE + rows].astype(bf16)
        for m in range(micro):
            low, high = both(m * EDGE, EDGE)
            field = jnp.concatenate([low, h[m], high], axis=0)
            agg = jnp.dot(gather, field, preferred_element_type=f32) * (1.0 / K)
            z_field = (field[HALO : HALO + span].astype(f32) + agg).astype(bf16)
            z_out[m] = z_field[HALO : HALO + rows]
            u = jnp.dot(z_field, w[...], preferred_element_type=f32)
            sig = 1.0 / (1.0 + jnp.exp(-u))
            factor[m] = sig * (1.0 + u * (1.0 - sig))


def layer_kernel(layer, m, fresh, flags, main, from_x, from_y, factor, mix, w_t, *refs):
    grads, kept, *sends = refs[0 if fresh else 2 :]
    micro, rows, _ = grads.shape

    @pl.when(flags[layer] == 1)
    def _():
        even = flags[EVEN] == 1
        if layer == 7:
            start = micro * EDGE + 16 + HALO * m
            own = main[m]
            x, y = (r[start : start + HALO, :] for r in (from_x, from_y))
        else:
            own, x, y = main[...], from_x[...], from_y[...]
        g_field = jnp.concatenate([jnp.where(even, y, x), own, jnp.where(even, x, y)], axis=0)
        du = (g_field.astype(f32) * factor[m]).astype(bf16)
        kept[m] = du[HALO : HALO + rows]
        mixed = jnp.dot(mix[...], du, preferred_element_type=f32)
        mixed = (mixed * (1.0 / K)).astype(bf16)
        dz = jnp.dot(mixed, w_t[...], preferred_element_type=f32)
        total = (own.astype(f32) + dz).astype(bf16)
        grads[m] = total
        if sends:
            upper, lower = total[rows - HALO :], total[:HALO]
            sends[0][...] = total
            sends[1][...] = jnp.where(even, upper, lower)
            sends[2][...] = jnp.where(even, lower, upper)


def split_kernel(flags, z, mine, other):
    micro, rows, width = z.shape
    z_t = z[...].reshape(micro * rows, width).T
    even = flags[EVEN] == 1
    for q in range(width // 32):
        a, b = z_t[32 * q : 32 * q + 16], z_t[32 * q + 16 : 32 * q + 32]
        mine[16 * q : 16 * q + 16, :] = jnp.where(even, a, b)
        other[16 * q : 16 * q + 16, :] = jnp.where(even, b, a)


def weight_kernel(flags, za, zb, da, db, out):
    micro, rows, width = da.shape
    total = jnp.dot(za[...], da[...].reshape(micro * rows, width), preferred_element_type=f32)
    total = total + jnp.dot(
        zb[...], db[...].reshape(micro * rows, width), preferred_element_type=f32
    )
    total = total.astype(bf16)
    for q in range(2 * out.shape[0]):
        y, z_hi, x = q // 8, (q // 4) % 2, q % 4
        out[4 * y + x, 16 * z_hi : 16 * z_hi + 16, :] = total[16 * q : 16 * q + 16]


def sum_kernel(flags, parts, mine, other):
    total = parts[0].astype(f32)
    for i in range(1, parts.shape[0]):
        total = total + parts[i].astype(f32)
    first = flags[LOWER] == 0
    a, b = total[:16], total[16:]
    mine[...] = jnp.where(first, a, b)
    other[...] = jnp.where(first, b, a)


def add_kernel(flags, a, b, out):
    out[...] = a[...] + b[...]


def shards(acts, upstream, weights, neighbours):
    sections = lax.axis_size("section")
    count = lax.axis_size("space")
    section = lax.axis_index("section")
    shard = lax.axis_index("space")
    rows = neighbours.shape[0]
    width = weights.shape[2]
    micro = upstream.shape[0]
    nodes = rows * count
    h, w = acts[0], weights[0]
    span = rows + 2 * HALO
    top = [sections - 1]
    near = [sections - 2, sections - 3]
    rest = list(range(sections - 3))

    near_by = jnp.logical_and(section >= near[-1], section < top[0])
    extra = [shard % 2 == 0, near_by, section < near[-1], (shard // 8) % 2 == 1]
    extra = jnp.stack([*(e.astype(jnp.int32) for e in extra), shard * rows, jnp.int32(nodes)])
    flags = jnp.concatenate([(section == jnp.arange(sections)).astype(jnp.int32), extra])

    def beside(which, j):
        return (j ^ 1) if which == 0 else (j - 1 if j % 2 == 0 else j + 1) % count

    def edges(which, senders, step):
        return [
            (s * count + j, (s - step) * count + beside(which, j)) for s in senders for j in range(count)
        ]

    def ahead(s):
        return [(s * count + j, (s - 1) * count + j) for j in range(count)]

    def swap(bit):
        return [(s * count + j, s * count + (j ^ bit)) for s in range(sections) for j in range(count)]

    short = ((micro * EDGE + 16, width), bf16)
    long = ((micro * (EDGE + HALO) + 16, width), bf16)
    off, tx, ty, x_pack, y_pack = call(
        pack_kernel,
        [((rows, 128), bf16), long, long, short, short],
        flags,
        [h, upstream, neighbours],
    )
    ty = permute(ty, edges(1, top, 0))
    tx = permute(tx, edges(0, top, 0))
    (w_t,) = call(turn_kernel, [((width, width), bf16)], flags, [w])
    field = ((micro, rows, width), bf16)
    made = [((micro, span, width), f32), ((rows, span), bf16), field]

    def prepare(active, sides, old=()):
        return call(
            functools.partial(prepare_kernel, active),
            made,
            flags,
            [h, off, w, *sides, *old],
            {6 + i: i for i in range(len(old))},
        )

    factor, mix, z = prepare(top[0], (tx, ty))

    grads = kept = None
    received = [[upstream, tx, ty]] * micro
    for layer in reversed(range(sections)):
        if layer in (near[0], near[-1]):
            _, active, group = ("near", NEAR, near) if layer == near[0] else ("rest", FAR, rest)
            x_pack, y_pack, factor, grads = lax.optimization_barrier((x_pack, y_pack, factor, grads))
            from_y = permute(y_pack, edges(1, group, 0))
            from_x = permute(x_pack, edges(0, group, 0))
            factor, mix, z = prepare(active, (from_x, from_y), (factor, mix, z))
        if layer == near[-1]:
            half_shape = ((width // 2, micro * rows), bf16)
            mine, other = call(split_kernel, [half_shape] * 2, flags, [z])
            other = permute(other, swap(1))
            grads, other = lax.optimization_barrier((grads, other))
        arriving = []
        for m in range(micro):
            fresh = grads is None
            sent = [((r, width), bf16) for r in (rows, HALO, HALO)] if layer else []
            grads, kept, *sends = call(
                functools.partial(layer_kernel, layer, m, fresh),
                [field, field, *sent],
                flags,
                [*received[m], factor, mix, w_t, *([] if fresh else [grads, kept])],
                {} if fresh else {7: 0, 8: 1},
            )
            if layer:
                y = permute(sends[2], edges(1, [layer], 1))
                main = permute(sends[0], ahead(layer))
                x = permute(sends[1], edges(0, [layer], 1))
                arriving.append([main, x, y])
        received = arriving

    du_other = permute(kept, swap(1))
    (partial,) = call(
        weight_kernel,
        [((count // 4, 2 * width // count, width), bf16)],
        flags,
        [mine, other, kept, du_other],
    )
    groups = [
        [16 * y + 8 * z + 2 * x + c for y in range(4) for x in range(4)]
        for z in range(2)
        for c in range(2)
    ]
    parts = lax.all_to_all(partial, "space", 0, 0, axis_index_groups=groups)
    slab = ((width // count, width), f32)
    mine, other = call(sum_kernel, [slab, slab], flags, [parts])
    other = permute(other, swap(8))
    (weight_grad,) = call(add_kernel, [slab], flags, [mine, other])
    return (grads[None], weight_grad[None])


def solution(mesh):
    in_specs = (
        P("section", None, "space", None),
        P(None, "space", None),
        P("section", None, None),
        P("space", None),
    )
    out_specs = (P("section", None, "space", None), P("section", "space", None))

    return jax.shard_map(shards, mesh=mesh, in_specs=in_specs, out_specs=out_specs, check_vma=False)
```

time: 1350 us -> 459 us (0.34)
  the two profiles are of different devices: /device:TPU:32 before, /device:TPU:3 now
where the time goes in v1:
time: 459 us; the launch traced here: 458 us
  starting transfers between devices  297 us (65%)
  waiting for transfers between devices  103 us (22%)
  blocking collectives  31.9 us (7%)
  Pallas kernels  18.5 us (4%)
  local copies, waits for them, and re-layouts  6.93 us (2%)
    ppermute x51, starting transfers between devices, permute(): return lax.ppermute(value, AXES, pairs)  297 us
    ppermute x51, waiting for transfers between devices, permute(): return lax.ppermute(value, AXES, pairs)  103 us
    all_to_all x1, blocking collectives, shards(): parts = lax.all_to_all(partial, 'space', 0, 0, axis_index_groups=groups)  31.9 us
    pallas_call x25, Pallas kernels, call(): pl.pallas_call(kernel, out_shape=tuple((pltpu.VMEM(shape, dtype) for shap...  18.5 us
  transfers between devices with their start and end apart: 51, of which 5 were waited for; matrix products, arithmetic and copies ran while one was open for 0% of the time, Pallas kernels for 2%

profile of v1, /device:TPU:3, one launch (start us, length us, event | category | flops | bytes accessed | tf_op | source)
XLA Modules:
  0.0 458.3 jit_solution(3604265095354175008)
XLA Ops:
  4.4 20.4 %collective-permute-start = (bf16[208,1024]{1,0:T(8,128)(2,1)S(1)}, bf16[208,1024]{1,0:T(8,128)(2,1)S(1)}, u32[]{:S(2)}, u32[]{:S(2)}) collective-permute-start(bf16[208,1024]{1,0:T(8,128)(2,1)S(1)} %get-tuple-element.104), channel_id=1, source_target_pairs={{448,449},{449,448},{450,451},{451,450},{452,453},{453,452},{454,4... | collective-permute-start | bytes 1277960 | tf_op jit(solution)/shard_map/ppermute | solution.py:29
  24.8 18.4 %collective-permute-start.1 = (bf16[208,1024]{1,0:T(8,128)(2,1)S(1)}, bf16[208,1024]{1,0:T(8,128)(2,1)S(1)}, u32[]{:S(2)}, u32[]{:S(2)}) collective-permute-start(bf16[208,1024]{1,0:T(8,128)(2,1)S(1)} %get-tuple-element.105), channel_id=1, source_target_pairs={{448,511},{449,450},{450,449},{451,452},{452,451},{453,454},{454,4... | collective-permute-start | bytes 1277960 | tf_op jit(solution)/shard_map/ppermute | solution.py:29
  43.3 1.6 copy-done
  48.7 25.8 %collective-permute-start.5 = (bf16[144,1024]{1,0:T(8,128)(2,1)S(1)}, bf16[144,1024]{1,0:T(8,128)(2,1)S(1)}, u32[]{:S(2)}, u32[]{:S(2)}) collective-permute-start(bf16[144,1024]{1,0:T(8,128)(2,1)S(1)} %get-tuple-element.134), channel_id=1, source_target_pairs={{384,385},{385,384},{386,387},{387,386},{388,389},{389,388},{390,3... | collective-permute-start | bytes 884744 | tf_op jit(solution)/shard_map/ppermute | solution.py:29
  74.5 18.4 %collective-permute-start.6 = (bf16[144,1024]{1,0:T(8,128)(2,1)S(1)}, bf16[144,1024]{1,0:T(8,128)(2,1)S(1)}, u32[]{:S(2)}, u32[]{:S(2)}) collective-permute-start(bf16[144,1024]{1,0:T(8,128)(2,1)S(1)} %get-tuple-element.135), channel_id=1, source_target_pairs={{384,447},{385,386},{386,385},{387,388},{388,387},{389,390},{390,3... | collective-permute-start | bytes 884744 | tf_op jit(solution)/shard_map/ppermute | solution.py:29
  92.9 18.4 %collective-permute-start.7 = (bf16[128,1024]{1,0:T(8,128)(2,1)S(1)}, bf16[128,1024]{1,0:T(8,128)(2,1)S(1)}, u32[]{:S(2)}, u32[]{:S(2)}) collective-permute-start(bf16[128,1024]{1,0:T(8,128)(2,1)S(1)} %get-tuple-element.123), channel_id=1, source_target_pairs={{448,384},{449,385},{450,386},{451,387},{452,388},{453,389},{454,3... | collective-permute-start | bytes 786440 | tf_op jit(solution)/shard_map/ppermute | solution.py:29
  111.3 18.4 %collective-permute-start.2 = (bf16[128,1024]{1,0:T(8,128)(2,1)S(1)}, bf16[128,1024]{1,0:T(8,128)(2,1)S(1)}, u32[]{:S(2)}, u32[]{:S(2)}) collective-permute-start(bf16[128,1024]{1,0:T(8,128)(2,1)S(1)} %get-tuple-element.111), channel_id=1, source_target_pairs={{448,384},{449,385},{450,386},{451,387},{452,388},{453,389},{454,3... | collective-permute-start | bytes 786440 | tf_op jit(solution)/shard_map/ppermute | solution.py:29
  130.4 23.9 %collective-permute-start.9 = (bf16[32,1024]{1,0:T(8,128)(2,1)S(1)}, bf16[32,1024]{1,0:T(8,128)(2,1)S(1)}, u32[]{:S(2)}, u32[]{:S(2)}) collective-permute-start(bf16[32,1024]{1,0:T(8,128)(2,1)S(1)} %get-tuple-element.125), channel_id=1, source_target_pairs={{448,447},{449,386},{450,385},{451,388},{452,387},{453,390},{454,3... | collective-permute-start | bytes 196616 | tf_op jit(solution)/shard_map/ppermute | solution.py:29
  154.9 18.4 %collective-permute-start.4 = (bf16[32,1024]{1,0:T(8,128)(2,1)S(1)}, bf16[32,1024]{1,0:T(8,128)(2,1)S(1)}, u32[]{:S(2)}, u32[]{:S(2)}) collective-permute-start(bf16[32,1024]{1,0:T(8,128)(2,1)S(1)} %get-tuple-element.113), channel_id=1, source_target_pairs={{448,447},{449,386},{450,385},{451,388},{452,387},{453,390},{454,3... | collective-permute-start | bytes 196616 | tf_op jit(solution)/shard_map/ppermute | solution.py:29
  175.0 22.0 %collective-permute-start.13 = (bf16[144,1024]{1,0:T(8,128)(2,1)S(1)}, bf16[144,1024]{1,0:T(8,128)(2,1)S(1)}, u32[]{:S(2)}, u32[]{:S(2)}) collective-permute-start(bf16[144,1024]{1,0:T(8,128)(2,1)S(1)} %get-tuple-element.134), channel_id=1, source_target_pairs={{0,1},{1,0},{2,3},{3,2},{4,5},{5,4},{6,7},{7,6},{8,9},{9,8},{10,11... | collective-permute-start | bytes 884744 | tf_op jit(solution)/shard_map/ppermute | solution.py:29
  197.0 19.0 %collective-permute-start.14 = (bf16[144,1024]{1,0:T(8,128)(2,1)S(1)}, bf16[144,1024]{1,0:T(8,128)(2,1)S(1)}, u32[]{:S(2)}, u32[]{:S(2)}) collective-permute-start(bf16[144,1024]{1,0:T(8,128)(2,1)S(1)} %get-tuple-element.135), channel_id=1, source_target_pairs={{0,63},{1,2},{2,1},{3,4},{4,3},{5,6},{6,5},{7,8},{8,7},{9,10},{10,... | collective-permute-start | bytes 884744 | tf_op jit(solution)/shard_map/ppermute | solution.py:29
  216.1 5.8 %collective-permute-done.14.from_y = bf16[144,1024]{1,0:T(8,128)(2,1)S(1)} collective-permute-done((bf16[144,1024]{1,0:T(8,128)(2,1)S(1)}, bf16[144,1024]{1,0:T(8,128)(2,1)S(1)}, u32[]{:S(2)}, u32[]{:S(2)}) %collective-permute-start.14) | collective-permute-done | bytes 294944 | tf_op jit(solution)/shard_map/ppermute | solution.py:29
  221.9 2.3 shard_map.67
  224.9 1.9 collective-permute-start.18
  228.9 23.4 %collective-permute-start.17 = (bf16[32,1024]{1,0:T(8,128)(2,1)S(1)}, bf16[32,1024]{1,0:T(8,128)(2,1)S(1)}, u32[]{:S(2)}, u32[]{:S(2)}) collective-permute-start(bf16[32,1024]{1,0:T(8,128)(2,1)S(1)} %get-tuple-element.142), channel_id=1, source_target_pairs={{384,383},{385,322},{386,321},{387,324},{388,323},{389,326},{390,3... | collective-permute-start | bytes 196616 | tf_op jit(solution)/shard_map/ppermute | solution.py:29
  253.0 18.4 %collective-permute-start.12 = (bf16[32,1024]{1,0:T(8,128)(2,1)S(1)}, bf16[32,1024]{1,0:T(8,128)(2,1)S(1)}, u32[]{:S(2)}, u32[]{:S(2)}) collective-permute-start(bf16[32,1024]{1,0:T(8,128)(2,1)S(1)} %get-tuple-element.132), channel_id=1, source_target_pairs={{384,383},{385,322},{386,321},{387,324},{388,323},{389,326},{390,3... | collective-permute-start | bytes 196616 | tf_op jit(solution)/shard_map/ppermute | solution.py:29
  293.1 1.3 collective-permute-start.46
  300.2 73.6 %collective-permute-done.47.from_x = bf16[32,1024]{1,0:T(8,128)(2,1)S(1)} collective-permute-done((bf16[32,1024]{1,0:T(8,128)(2,1)S(1)}, bf16[32,1024]{1,0:T(8,128)(2,1)S(1)}, u32[]{:S(2)}, u32[]{:S(2)}) %collective-permute-start.47) | collective-permute-done | bytes 65568 | tf_op jit(solution)/shard_map/ppermute | solution.py:29
  376.3 4.0 collective-permute-done.45.from_y
  381.4 1.9 collective-permute-start.49
  383.4 1.9 collective-permute-done.49.db
  386.5 31.9 %all_to_all.5.parts = bf16[16,32,1024]{2,1,0:T(8,128)(2,1)S(1)} all-to-all(bf16[16,32,1024]{2,1,0:T(8,128)(2,1)S(1)} %shard_map.81), channel_id=1, replica_groups={{0,2,4,6,16,18,20,22,32,34,36,38,48,50,52,54},{1,3,5,7,17,19,21,23,33,3..., dimensions={0} | all-to-all | bytes 2097152 | tf_op jit(solution)/shard_map/all_to_all | solution.py:280
  419.1 20.0 %collective-permute-start.50 = (f32[16,1024]{1,0:T(8,128)S(1)}, f32[16,1024]{1,0:T(8,128)S(1)}, u32[]{:S(2)}, u32[]{:S(2)}) collective-permute-start(f32[16,1024]{1,0:T(8,128)S(1)} %get-tuple-element.205), channel_id=1, source_target_pairs={{0,8},{1,9},{2,10},{3,11},{4,12},{5,13},{6,14},{7,15},{8,0},{9,1},... | collective-permute-start | bytes 196616 | tf_op jit(solution)/shard_map/ppermute | solution.py:29
  439.8 17.3 %collective-permute-done.50.b = f32[16,1024]{1,0:T(8,128)S(1)} collective-permute-done((f32[16,1024]{1,0:T(8,128)S(1)}, f32[16,1024]{1,0:T(8,128)S(1)}, u32[]{:S(2)}, u32[]{:S(2)}) %collective-permute-start.50) | collective-permute-done | bytes 65568 | tf_op jit(solution)/shard_map/ppermute | solution.py:29
  (121 shorter events, 48.4 us)
Async XLA Ops:
  4.4 41.6 %collective-permute-start = (bf16[208,1024]{1,0:T(8,128)(2,1)S(1)}, bf16[208,1024]{1,0:T(8,128)(2,1)S(1)}, u32[]{:S(2)}, u32[]{:S(2)}) collective-permute-start(bf16[208,1024]{1,0:T(8,128)(2,1)S(1)} %get-tuple-element.104), channel_id=1, source_target_pairs={{448,449},{449,448},{450,451},{451,450},{452,453},{453,452},{454,4... | collective-permute-start | bytes 1277960 | tf_op jit(solution)/shard_map/ppermute | solution.py:29
  24.8 21.2 %collective-permute-start.1 = (bf16[208,1024]{1,0:T(8,128)(2,1)S(1)}, bf16[208,1024]{1,0:T(8,128)(2,1)S(1)}, u32[]{:S(2)}, u32[]{:S(2)}) collective-permute-start(bf16[208,1024]{1,0:T(8,128)(2,1)S(1)} %get-tuple-element.105), channel_id=1, source_target_pairs={{448,511},{449,450},{450,449},{451,452},{452,451},{453,454},{454,4... | collective-permute-start | bytes 1277960 | tf_op jit(solution)/shard_map/ppermute | solution.py:29
  48.7 105.6 %collective-permute-start.5 = (bf16[144,1024]{1,0:T(8,128)(2,1)S(1)}, bf16[144,1024]{1,0:T(8,128)(2,1)S(1)}, u32[]{:S(2)}, u32[]{:S(2)}) collective-permute-start(bf16[144,1024]{1,0:T(8,128)(2,1)S(1)} %get-tuple-element.134), channel_id=1, source_target_pairs={{384,385},{385,384},{386,387},{387,386},{388,389},{389,388},{390,3... | collective-permute-start | bytes 884744 | tf_op jit(solution)/shard_map/ppermute | solution.py:29
  74.5 80.4 %collective-permute-start.6 = (bf16[144,1024]{1,0:T(8,128)(2,1)S(1)}, bf16[144,1024]{1,0:T(8,128)(2,1)S(1)}, u32[]{:S(2)}, u32[]{:S(2)}) collective-permute-start(bf16[144,1024]{1,0:T(8,128)(2,1)S(1)} %get-tuple-element.135), channel_id=1, source_target_pairs={{384,447},{385,386},{386,385},{387,388},{388,387},{389,390},{390,3... | collective-permute-start | bytes 884744 | tf_op jit(solution)/shard_map/ppermute | solution.py:29
  92.9 81.0 %collective-permute-start.7 = (bf16[128,1024]{1,0:T(8,128)(2,1)S(1)}, bf16[128,1024]{1,0:T(8,128)(2,1)S(1)}, u32[]{:S(2)}, u32[]{:S(2)}) collective-permute-start(bf16[128,1024]{1,0:T(8,128)(2,1)S(1)} %get-tuple-element.123), channel_id=1, source_target_pairs={{448,384},{449,385},{450,386},{451,387},{452,388},{453,389},{454,3... | collective-permute-start | bytes 786440 | tf_op jit(solution)/shard_map/ppermute | solution.py:29
  111.3 63.2 %collective-permute-start.2 = (bf16[128,1024]{1,0:T(8,128)(2,1)S(1)}, bf16[128,1024]{1,0:T(8,128)(2,1)S(1)}, u32[]{:S(2)}, u32[]{:S(2)}) collective-permute-start(bf16[128,1024]{1,0:T(8,128)(2,1)S(1)} %get-tuple-element.111), channel_id=1, source_target_pairs={{448,384},{449,385},{450,386},{451,387},{452,388},{453,389},{454,3... | collective-permute-start | bytes 786440 | tf_op jit(solution)/shard_map/ppermute | solution.py:29
  130.4 43.5 %collective-permute-start.9 = (bf16[32,1024]{1,0:T(8,128)(2,1)S(1)}, bf16[32,1024]{1,0:T(8,128)(2,1)S(1)}, u32[]{:S(2)}, u32[]{:S(2)}) collective-permute-start(bf16[32,1024]{1,0:T(8,128)(2,1)S(1)} %get-tuple-element.125), channel_id=1, source_target_pairs={{448,447},{449,386},{450,385},{451,388},{452,387},{453,390},{454,3... | collective-permute-start | bytes 196616 | tf_op jit(solution)/shard_map/ppermute | solution.py:29
  154.3 20.2 %collective-permute-start.3 = (bf16[32,1024]{1,0:T(8,128)(2,1)S(1)}, bf16[32,1024]{1,0:T(8,128)(2,1)S(1)}, u32[]{:S(2)}, u32[]{:S(2)}) collective-permute-start(bf16[32,1024]{1,0:T(8,128)(2,1)S(1)} %get-tuple-element.112), channel_id=1, source_target_pairs={{448,385},{449,384},{450,387},{451,386},{452,389},{453,388},{454,3... | collective-permute-start | bytes 196616 | tf_op jit(solution)/shard_map/ppermute | solution.py:29
  154.9 19.5 %collective-permute-start.4 = (bf16[32,1024]{1,0:T(8,128)(2,1)S(1)}, bf16[32,1024]{1,0:T(8,128)(2,1)S(1)}, u32[]{:S(2)}, u32[]{:S(2)}) collective-permute-start(bf16[32,1024]{1,0:T(8,128)(2,1)S(1)} %get-tuple-element.113), channel_id=1, source_target_pairs={{448,447},{449,386},{450,385},{451,388},{452,387},{453,390},{454,3... | collective-permute-start | bytes 196616 | tf_op jit(solution)/shard_map/ppermute | solution.py:29
  175.0 41.0 %collective-permute-start.13 = (bf16[144,1024]{1,0:T(8,128)(2,1)S(1)}, bf16[144,1024]{1,0:T(8,128)(2,1)S(1)}, u32[]{:S(2)}, u32[]{:S(2)}) collective-permute-start(bf16[144,1024]{1,0:T(8,128)(2,1)S(1)} %get-tuple-element.134), channel_id=1, source_target_pairs={{0,1},{1,0},{2,3},{3,2},{4,5},{5,4},{6,7},{7,6},{8,9},{9,8},{10,11... | collective-permute-start | bytes 884744 | tf_op jit(solution)/shard_map/ppermute | solution.py:29
  197.0 24.9 %collective-permute-start.14 = (bf16[144,1024]{1,0:T(8,128)(2,1)S(1)}, bf16[144,1024]{1,0:T(8,128)(2,1)S(1)}, u32[]{:S(2)}, u32[]{:S(2)}) collective-permute-start(bf16[144,1024]{1,0:T(8,128)(2,1)S(1)} %get-tuple-element.135), channel_id=1, source_target_pairs={{0,63},{1,2},{2,1},{3,4},{4,3},{5,6},{6,5},{7,8},{8,7},{9,10},{10,... | collective-permute-start | bytes 884744 | tf_op jit(solution)/shard_map/ppermute | solution.py:29
  224.9 28.1 %collective-permute-start.18 = (bf16[512,256]{1,0:T(8,128)(2,1)S(1)}, bf16[512,256]{1,0:T(8,128)(2,1)S(1)}, u32[]{:S(2)}, u32[]{:S(2)}) collective-permute-start(bf16[512,256]{1,0:T(8,128)(2,1)S(1)} %get-tuple-element.145), channel_id=1, source_target_pairs={{0,1},{1,0},{2,3},{3,2},{4,5},{5,4},{6,7},{7,6},{8,9},{9,8},{10,11... | collective-permute-start | bytes 786440 | tf_op jit(solution)/shard_map/ppermute | solution.py:29
  226.8 44.5 %collective-permute-start.15 = (bf16[128,1024]{1,0:T(8,128)(2,1)S(1)}, bf16[128,1024]{1,0:T(8,128)(2,1)S(1)}, u32[]{:S(2)}, u32[]{:S(2)}) collective-permute-start(bf16[128,1024]{1,0:T(8,128)(2,1)S(1)} %get-tuple-element.140), channel_id=1, source_target_pairs={{384,320},{385,321},{386,322},{387,323},{388,324},{389,325},{390,3... | collective-permute-start | bytes 786440 | tf_op jit(solution)/shard_map/ppermute | solution.py:29
  227.5 45.1 %collective-permute-start.10 = (bf16[128,1024]{1,0:T(8,128)(2,1)S(1)}, bf16[128,1024]{1,0:T(8,128)(2,1)S(1)}, u32[]{:S(2)}, u32[]{:S(2)}) collective-permute-start(bf16[128,1024]{1,0:T(8,128)(2,1)S(1)} %get-tuple-element.130), channel_id=1, source_target_pairs={{384,320},{385,321},{386,322},{387,323},{388,324},{389,325},{390,3... | collective-permute-start | bytes 786440 | tf_op jit(solution)/shard_map/ppermute | solution.py:29
  228.2 24.1 %collective-permute-start.16 = (bf16[32,1024]{1,0:T(8,128)(2,1)S(1)}, bf16[32,1024]{1,0:T(8,128)(2,1)S(1)}, u32[]{:S(2)}, u32[]{:S(2)}) collective-permute-start(bf16[32,1024]{1,0:T(8,128)(2,1)S(1)} %get-tuple-element.141), channel_id=1, source_target_pairs={{384,321},{385,320},{386,323},{387,322},{388,325},{389,324},{390,3... | collective-permute-start | bytes 196616 | tf_op jit(solution)/shard_map/ppermute | solution.py:29
  228.9 42.5 %collective-permute-start.17 = (bf16[32,1024]{1,0:T(8,128)(2,1)S(1)}, bf16[32,1024]{1,0:T(8,128)(2,1)S(1)}, u32[]{:S(2)}, u32[]{:S(2)}) collective-permute-start(bf16[32,1024]{1,0:T(8,128)(2,1)S(1)} %get-tuple-element.142), channel_id=1, source_target_pairs={{384,383},{385,322},{386,321},{387,324},{388,323},{389,326},{390,3... | collective-permute-start | bytes 196616 | tf_op jit(solution)/shard_map/ppermute | solution.py:29
  252.3 20.3 %collective-permute-start.11 = (bf16[32,1024]{1,0:T(8,128)(2,1)S(1)}, bf16[32,1024]{1,0:T(8,128)(2,1)S(1)}, u32[]{:S(2)}, u32[]{:S(2)}) collective-permute-start(bf16[32,1024]{1,0:T(8,128)(2,1)S(1)} %get-tuple-element.131), channel_id=1, source_target_pairs={{384,321},{385,320},{386,323},{387,322},{388,325},{389,324},{390,3... | collective-permute-start | bytes 196616 | tf_op jit(solution)/shard_map/ppermute | solution.py:29
  253.0 19.6 %collective-permute-start.12 = (bf16[32,1024]{1,0:T(8,128)(2,1)S(1)}, bf16[32,1024]{1,0:T(8,128)(2,1)S(1)}, u32[]{:S(2)}, u32[]{:S(2)}) collective-permute-start(bf16[32,1024]{1,0:T(8,128)(2,1)S(1)} %get-tuple-element.132), channel_id=1, source_target_pairs={{384,383},{385,322},{386,321},{387,324},{388,323},{389,326},{390,3... | collective-permute-start | bytes 196616 | tf_op jit(solution)/shard_map/ppermute | solution.py:29
  293.1 82.0 %collective-permute-start.46 = (bf16[128,1024]{1,0:T(8,128)(2,1)S(1)}, bf16[128,1024]{1,0:T(8,128)(2,1)S(1)}, u32[]{:S(2)}, u32[]{:S(2)}) collective-permute-start(bf16[128,1024]{1,0:T(8,128)(2,1)S(1)} %get-tuple-element.193), channel_id=1, source_target_pairs={{64,0},{65,1},{66,2},{67,3},{68,4},{69,5},{70,6},{71,7},{72,8},{73... | collective-permute-start | bytes 786440 | tf_op jit(solution)/shard_map/ppermute | solution.py:29
  295.0 85.3 %collective-permute-start.43 = (bf16[128,1024]{1,0:T(8,128)(2,1)S(1)}, bf16[128,1024]{1,0:T(8,128)(2,1)S(1)}, u32[]{:S(2)}, u32[]{:S(2)}) collective-permute-start(bf16[128,1024]{1,0:T(8,128)(2,1)S(1)} %get-tuple-element.190), channel_id=1, source_target_pairs={{64,0},{65,1},{66,2},{67,3},{68,4},{69,5},{70,6},{71,7},{72,8},{73... | collective-permute-start | bytes 786440 | tf_op jit(solution)/shard_map/ppermute | solution.py:29
  296.3 77.5 %collective-permute-start.47 = (bf16[32,1024]{1,0:T(8,128)(2,1)S(1)}, bf16[32,1024]{1,0:T(8,128)(2,1)S(1)}, u32[]{:S(2)}, u32[]{:S(2)}) collective-permute-start(bf16[32,1024]{1,0:T(8,128)(2,1)S(1)} %get-tuple-element.194), channel_id=1, source_target_pairs={{64,1},{65,0},{66,3},{67,2},{68,5},{69,4},{70,7},{71,6},{72,9},{73... | collective-permute-start | bytes 196616 | tf_op jit(solution)/shard_map/ppermute | solution.py:29
  297.6 77.5 %collective-permute-start.48 = (bf16[32,1024]{1,0:T(8,128)(2,1)S(1)}, bf16[32,1024]{1,0:T(8,128)(2,1)S(1)}, u32[]{:S(2)}, u32[]{:S(2)}) collective-permute-start(bf16[32,1024]{1,0:T(8,128)(2,1)S(1)} %get-tuple-element.195), channel_id=1, source_target_pairs={{64,63},{65,2},{66,1},{67,4},{68,3},{69,6},{70,5},{71,8},{72,7},{7... | collective-permute-start | bytes 196616 | tf_op jit(solution)/shard_map/ppermute | solution.py:29
  298.9 77.4 %collective-permute-start.44 = (bf16[32,1024]{1,0:T(8,128)(2,1)S(1)}, bf16[32,1024]{1,0:T(8,128)(2,1)S(1)}, u32[]{:S(2)}, u32[]{:S(2)}) collective-permute-start(bf16[32,1024]{1,0:T(8,128)(2,1)S(1)} %get-tuple-element.191), channel_id=1, source_target_pairs={{64,1},{65,0},{66,3},{67,2},{68,5},{69,4},{70,7},{71,6},{72,9},{73... | collective-permute-start | bytes 196616 | tf_op jit(solution)/shard_map/ppermute | solution.py:29
  419.1 38.1 %collective-permute-start.50 = (f32[16,1024]{1,0:T(8,128)S(1)}, f32[16,1024]{1,0:T(8,128)S(1)}, u32[]{:S(2)}, u32[]{:S(2)}) collective-permute-start(f32[16,1024]{1,0:T(8,128)S(1)} %get-tuple-element.205), channel_id=1, source_target_pairs={{0,8},{1,9},{2,10},{3,11},{4,12},{5,13},{6,14},{7,15},{8,0},{9,1},... | collective-permute-start | bytes 196616 | tf_op jit(solution)/shard_map/ppermute | solution.py:29
  (33 other events, 93.6 us)

commit v2 on v1

v2 whole, which is shorter than its diff:
```python
import functools

import jax
import jax.numpy as jnp
from jax import lax
from jax.experimental import pallas as pl
from jax.experimental.pallas import tpu as pltpu
from jax.sharding import PartitionSpec as P


K = 6
HALO = 32
EDGE = 2 * HALO
WIDE = 3 * HALO
AXES = ("section", "space")

bf16 = jnp.bfloat16
f32 = jnp.float32
VMEM = pl.BlockSpec(memory_space=pltpu.VMEM)
SMEM = pl.BlockSpec(memory_space=pltpu.SMEM)
LIMIT = pltpu.CompilerParams(vmem_limit_bytes=16 * 1024 * 1024)
EVEN, REST, LOWER, BASE, NODES = 8, 9, 10, 11, 12


def on_chip(value):
    return pltpu.with_memory_space_constraint(value, pltpu.VMEM)


def permute(value, pairs):
    return lax.ppermute(value, AXES, pairs)


def call(kernel, outs, flags, arrays, aliases=None):
    return pl.pallas_call(
        kernel,
        out_shape=tuple(pltpu.VMEM(shape, dtype) for shape, dtype in outs),
        in_specs=[SMEM] + [VMEM] * len(arrays),
        out_specs=tuple([VMEM] * len(outs)),
        input_output_aliases=aliases or {},
        compiler_params=LIMIT,
    )(flags, *[on_chip(a) for a in arrays])


def turn_kernel(flags, w, out):
    out[...] = w[...].T


def pack_kernel(flags, h, up, neighbours, off, *edges):
    micro, rows, width = h.shape
    nodes = flags[NODES]
    even = flags[EVEN] == 1
    ids = flags[BASE] + lax.broadcasted_iota(jnp.int32, neighbours.shape, 0)
    step = neighbours[...] - ids
    step = jnp.where(step > HALO, step - nodes, step)
    step = jnp.where(step < -HALO, step + nodes, step)
    off[...] = jnp.zeros(off.shape, bf16)
    off[:, :K] = step.astype(f32).astype(bf16)
    blank = jnp.zeros((16, width - 512), bf16)

    def edge(upper):
        def cut(value, size):
            return value[rows - size :] if upper else value[:size]

        steps = cut(off, EDGE)
        steps = jnp.concatenate([*[steps[16 * p : 16 * p + 16] for p in range(4)], blank], axis=1)
        inner = [cut(h[m], WIDE) for m in range(micro)] + [steps]
        return jnp.concatenate(inner + [cut(up[m], EDGE) for m in range(micro)], axis=0)

    lower, upper = edge(False), edge(True)
    x, y = jnp.where(even, upper, lower), jnp.where(even, lower, upper)
    for value, full, short in ((x, edges[0], edges[2]), (y, edges[1], edges[3])):
        full[...] = value
        short[...] = value[: short.shape[0]]


def slope(u):
    sig = 1.0 / (1.0 + jnp.exp(-u))
    return sig * (1.0 + u * (1.0 - sig))


def prepare_kernel(active, flags, h, off, w, from_x, from_y, *refs):
    factor, mix, z_out = refs[-3:]
    micro, rows, width = h.shape
    span = rows + 2 * EDGE
    reach = rows + 2 * WIDE
    lanes = -(-reach // 128) * 128

    @pl.when(flags[active] == 1)
    def _():
        even = flags[EVEN] == 1

        def both(start, size):
            x, y = from_x[start : start + size, :], from_y[start : start + size, :]
            return jnp.where(even, y, x), jnp.where(even, x, y)

        low, high = both(micro * WIDE, 16)
        cut = [slice(128 * p, 128 * p + 128) for p in range(EDGE // 16)]
        steps = jnp.concatenate(
            [*[low[:, c] for c in cut], off[...], *[high[:, c] for c in cut]], axis=0
        ).astype(f32)
        column = lax.broadcasted_iota(jnp.int32, (span, lanes), 1).astype(f32)
        row = lax.broadcasted_iota(jnp.int32, (span, lanes), 0).astype(f32)
        distance = column - row - float(HALO)
        count = jnp.zeros((span, lanes), f32)
        for k in range(K):
            count = count + jnp.where(distance == steps[:, k : k + 1], 1.0, 0.0)
        gather = count.astype(bf16)
        mix[...] = (count + jnp.where(distance == 0.0, float(K), 0.0)).T[:reach].astype(bf16)
        blank = jnp.zeros((lanes - reach, width), bf16)
        for m in range(micro):
            low, high = both(m * WIDE, WIDE)
            field = jnp.concatenate([low, h[m], high, blank], axis=0)
            agg = jnp.dot(gather, field, preferred_element_type=f32) * (1.0 / K)
            z_field = (field[HALO : HALO + span].astype(f32) + agg).astype(bf16)
            z_out[m] = z_field[EDGE : EDGE + rows]
            factor[m] = slope(jnp.dot(z_field, w[...], preferred_element_type=f32))


def layer_kernel(layer, m, sources, olds, flags, *refs):
    g_in = refs[:sources]
    factor, mix, w_t = refs[sources : sources + 3]
    grads, kept, *sends = refs[sources + 3 + olds :]
    micro, rows, width = grads.shape
    span = rows + EDGE
    odd = layer % 2 == 1

    @pl.when(flags[layer] == 1)
    def _():
        if layer == 7:
            start = micro * WIDE + 16 + EDGE * m
            x, y = (r[start : start + EDGE, :] for r in g_in[1:])
            own, edge = g_in[0][m], jnp.where(flags[EVEN] == 1, x, y)
        else:
            own, edge = g_in[0][...], g_in[1][...]
        g_field = jnp.concatenate([own, edge] if odd else [edge, own], axis=0)
        first = EDGE if odd else HALO
        du = (g_field.astype(f32) * factor[m, first : first + span, :]).astype(bf16)
        kept[m] = du[EDGE - first : EDGE - first + rows]
        blank = [jnp.zeros((n, width), bf16) for n in (first, mix.shape[1] - span - first)]
        parts = [p for p in (blank[0], du, blank[1]) if p.shape[0]]
        above = WIDE + (HALO if odd else 0)
        mixed = jnp.dot(
            mix[above : above + rows, :], jnp.concatenate(parts, axis=0), preferred_element_type=f32
        )
        mixed = (mixed * (1.0 / K)).astype(bf16)
        dz = jnp.dot(mixed, w_t[...], preferred_element_type=f32)
        total = (g_field[HALO : HALO + rows].astype(f32) + dz).astype(bf16)
        grads[m] = total
        if sends:
            sends[0][...] = total
            sends[1][...] = total[rows - EDGE :] if odd else total[:EDGE]


def rim_kernel(flags, grads, out):
    out[...] = grads[:, grads.shape[1] - HALO :, :]


def shift_kernel(flags, grads, rim, out):
    micro, rows, _ = grads.shape
    odd = flags[1] + flags[3] + flags[5] + flags[7] == 1
    for m in range(micro):
        moved = jnp.concatenate([rim[m], grads[m, : rows - HALO, :]], axis=0)
        out[m] = jnp.where(odd, moved, grads[m])


def split_kernel(flags, z, mine, other):
    micro, rows, width = z.shape
    z_t = z[...].reshape(micro * rows, width).T
    even = flags[EVEN] == 1
    for q in range(width // 32):
        a, b = z_t[32 * q : 32 * q + 16], z_t[32 * q + 16 : 32 * q + 32]
        mine[16 * q : 16 * q + 16, :] = jnp.where(even, a, b)
        other[16 * q : 16 * q + 16, :] = jnp.where(even, b, a)


def weight_kernel(flags, za, zb, da, db, out):
    micro, rows, width = da.shape
    total = jnp.dot(za[...], da[...].reshape(micro * rows, width), preferred_element_type=f32)
    total = total + jnp.dot(
        zb[...], db[...].reshape(micro * rows, width), preferred_element_type=f32
    )
    total = total.astype(bf16)
    for q in range(2 * out.shape[0]):
        y, z_hi, x = q // 8, (q // 4) % 2, q % 4
        out[4 * y + x, 16 * z_hi : 16 * z_hi + 16, :] = total[16 * q : 16 * q + 16]


def sum_kernel(flags, parts, mine, other):
    total = parts[0].astype(f32)
    for i in range(1, parts.shape[0]):
        total = total + parts[i].astype(f32)
    first = flags[LOWER] == 0
    a, b = total[:16], total[16:]
    mine[...] = jnp.where(first, a, b)
    other[...] = jnp.where(first, b, a)


def add_kernel(flags, a, b, out):
    out[...] = a[...] + b[...]


def shards(acts, upstream, weights, neighbours):
    sections = lax.axis_size("section")
    count = lax.axis_size("space")
    section = lax.axis_index("section")
    shard = lax.axis_index("space")
    rows = neighbours.shape[0]
    width = weights.shape[2]
    micro = upstream.shape[0]
    nodes = rows * count
    h, w = acts[0], weights[0]
    span = rows + 2 * EDGE
    reach = rows + 2 * WIDE
    top = [sections - 1]
    rest = list(range(sections - 1))

    extra = [shard % 2 == 0, section < top[0]]
    extra.append((shard // 8) % 2 == 1)
    extra = jnp.stack([*(e.astype(jnp.int32) for e in extra), shard * rows, jnp.int32(nodes)])
    flags = jnp.concatenate([(section == jnp.arange(sections)).astype(jnp.int32), extra])

    def beside(which, j):
        return (j ^ 1) if which == 0 else (j - 1 if j % 2 == 0 else j + 1) % count

    def edges(which, senders, step):
        return [
            (s * count + j, (s - step) * count + beside(which, j)) for s in senders for j in range(count)
        ]

    def toward(senders, step, side):
        return [(s * count + j, (s - step) * count + (j + side) % count) for s in senders for j in range(count)]

    def swap(bit):
        return [(s * count + j, s * count + (j ^ bit)) for s in range(sections) for j in range(count)]

    short = ((micro * WIDE + 16, width), bf16)
    long = ((micro * (WIDE + EDGE) + 16, width), bf16)
    off, tx, ty, x_pack, y_pack = call(
        pack_kernel,
        [((rows, 128), bf16), long, long, short, short],
        flags,
        [h, upstream, neighbours],
    )
    ty = permute(ty, edges(1, top, 0))
    tx = permute(tx, edges(0, top, 0))
    (w_t,) = call(turn_kernel, [((width, width), bf16)], flags, [w])
    field = ((micro, rows, width), bf16)
    made = [((micro, span, width), f32), ((reach, span), bf16), field]

    def prepare(active, sides, old=()):
        return call(
            functools.partial(prepare_kernel, active),
            made,
            flags,
            [h, off, w, *sides, *old],
            {6 + i: i for i in range(len(old))},
        )

    prepared = prepare(top[0], (tx, ty))
    grads = kept = None
    received = [[upstream, tx, ty]] * micro
    for layer in reversed(range(sections)):
        if layer == rest[-1]:
            x_pack, y_pack, grads, *prepared = lax.optimization_barrier(
                (x_pack, y_pack, grads, *prepared)
            )
            ry = permute(y_pack, edges(1, rest, 0))
            rx = permute(x_pack, edges(0, rest, 0))
            prepared = prepare(REST, (rx, ry), prepared)
        if layer == rest[-1] - 1:
            half_shape = ((width // 2, micro * rows), bf16)
            grads, z = lax.optimization_barrier((grads, prepared[2]))
            mine, other = call(split_kernel, [half_shape] * 2, flags, [z])
            other = permute(other, swap(1))
            grads, other = lax.optimization_barrier((grads, other))
        factor, mix, _ = prepared
        arriving = []
        for m in range(micro):
            old = [] if grads is None else [grads, kept]
            sent = [((r, width), bf16) for r in (rows, EDGE)] if layer else []
            first = 4 + len(received[m])
            grads, kept, *sends = call(
                functools.partial(layer_kernel, layer, m, len(received[m]), len(old)),
                [field, field, *sent],
                flags,
                [*received[m], factor, mix, w_t, *old],
                {first + i: i for i in range(len(old))},
            )
            if layer:
                side = 1 if layer % 2 else -1
                edge = permute(sends[1], toward([layer], 1, side))
                main = permute(sends[0], toward([layer], 1, 0))
                arriving.append([main, edge])
        received = arriving
        if layer == 1:
            (rim,) = call(rim_kernel, [((micro, HALO, width), bf16)], flags, [grads])
            rim = permute(rim, toward(range(1, sections, 2), 0, 1))

    du_other = permute(kept, swap(1))
    (partial,) = call(
        weight_kernel,
        [((count // 4, 2 * width // count, width), bf16)],
        flags,
        [mine, other, kept, du_other],
    )
    groups = [
        [16 * y + 8 * z + 2 * x + c for y in range(4) for x in range(4)]
        for z in range(2)
        for c in range(2)
    ]
    parts = lax.all_to_all(partial, "space", 0, 0, axis_index_groups=groups)
    slab = ((width // count, width), f32)
    mine, other = call(sum_kernel, [slab, slab], flags, [parts])
    other = permute(other, swap(8))
    (weight_grad,) = call(add_kernel, [slab], flags, [mine, other])
    (grads,) = call(shift_kernel, [field], flags, [grads, rim])
    return (grads[None], weight_grad[None])


def solution(mesh):
    in_specs = (
        P("section", None, "space", None),
        P(None, "space", None),
        P("section", None, None),
        P("space", None),
    )
    out_specs = (P("section", None, "space", None), P("section", "space", None))

    return jax.shard_map(shards, mesh=mesh, in_specs=in_specs, out_specs=out_specs, check_vma=False)
```

time: 459 us -> 224 us (0.49)
  the two profiles are of different devices: /device:TPU:3 before, /device:TPU:1 now
where the time goes in v2:
time: 224 us; the launch traced here: 223 us
  waiting for transfers between devices  121 us (54%)
  starting transfers between devices  73.1 us (33%)
  Pallas kernels  21.2 us (9%)
  local copies, waits for them, and re-layouts  6.58 us (3%)
    ppermute x36, waiting for transfers between devices, permute(): return lax.ppermute(value, AXES, pairs)  103 us
    ppermute x36, starting transfers between devices, permute(): return lax.ppermute(value, AXES, pairs)  69.5 us
    pallas_call x26, Pallas kernels, call(): pl.pallas_call(kernel, out_shape=tuple((pltpu.VMEM(shape, dtype) for shap...  21.2 us
    all_to_all x1, waiting for transfers between devices, shards(): parts = lax.all_to_all(partial, 'space', 0, 0, axis_index_groups=groups)  17.6 us
    unnamed x15, local copies, waits for them, and re-layouts  6.5 us
  transfers between devices with their start and end apart: 37, of which 6 were waited for; matrix products, arithmetic and copies ran while one was open for 0% of the time, Pallas kernels for 6%

profile of v2, /device:TPU:1, one launch (start us, length us, event | category | flops | bytes accessed | tf_op | source)
XLA Modules:
  0.0 223.4 jit_solution(5016349892867195510)
XLA Ops:
  1.6 1.0 copy-done.2
  2.6 1.0 copy-done.4
  3.7 0.9 shard_map.59
  6.0 1.6 copy-done
  7.6 1.2 shard_map.61.refs_5_.refs_4_
  11.1 8.7 %collective-permute-start.4 = (bf16[208,1024]{1,0:T(8,128)(2,1)S(1)}, bf16[208,1024]{1,0:T(8,128)(2,1)S(1)}, u32[]{:S(2)}, u32[]{:S(2)}) collective-permute-start(bf16[208,1024]{1,0:T(8,128)(2,1)S(1)} %get-tuple-element.100), channel_id=1, source_target_pairs={{0,1},{1,0},{2,3},{3,2},{4,5},{5,4},{6,7},{7,6},{8,9},{9,8},{10,11... | collective-permute-start | bytes 1277960 | tf_op jit(solution)/shard_map/ppermute | solution.py:30
  19.8 1.9 collective-permute-start.5
  24.5 4.8 %collective-permute-done.5.from_y = bf16[208,1024]{1,0:T(8,128)(2,1)S(1)} collective-permute-done((bf16[208,1024]{1,0:T(8,128)(2,1)S(1)}, bf16[208,1024]{1,0:T(8,128)(2,1)S(1)}, u32[]{:S(2)}, u32[]{:S(2)}) %collective-permute-start.5) | collective-permute-done | bytes 426016 | tf_op jit(solution)/shard_map/ppermute | solution.py:30
  29.3 3.1 %shard_map.64 = (f32[2,256,1024]{2,1,0:T(8,128)S(1)}, bf16[320,256]{1,0:T(8,128)(2,1)S(1)}, bf16[2,128,1024]{2,1,0:T(8,128)(2,1)S(1)}) custom-call(s32[13]{0:T(128)S(1)} %concatenate.3.flags, bf16[2,128,1024]{2,1,0:T(8,128)(2,1)S(1)} %bitcast.15, ...), custom_call_target="tpu_custom_call", output_to_operand_aliasing={{0}: (6, {}), {1}: (7, {}), {2}: (8, {})} | custom-call | tf_op jit(solution)/shard_map/pallas_call | solution.py:34
  34.2 26.2 %collective-permute-start.12 = (bf16[512,256]{1,0:T(8,128)(2,1)S(1)}, bf16[512,256]{1,0:T(8,128)(2,1)S(1)}, u32[]{:S(2)}, u32[]{:S(2)}) collective-permute-start(bf16[512,256]{1,0:T(8,128)(2,1)S(1)} %get-tuple-element.121), channel_id=1, source_target_pairs={{0,1},{1,0},{2,3},{3,2},{4,5},{5,4},{6,7},{7,6},{8,9},{9,8},{10,11... | collective-permute-start | bytes 786440 | tf_op jit(solution)/shard_map/ppermute | solution.py:30
  79.5 1.3 collective-permute-start.31
  81.3 1.3 collective-permute-start.29
  82.6 1.3 collective-permute-start.32
  83.9 1.3 collective-permute-start.30
  85.8 91.4 %collective-permute-done.32.refs_1_ = bf16[64,1024]{1,0:T(8,128)(2,1)S(1)} collective-permute-done((bf16[64,1024]{1,0:T(8,128)(2,1)S(1)}, bf16[64,1024]{1,0:T(8,128)(2,1)S(1)}, u32[]{:S(2)}, u32[]{:S(2)}) %collective-permute-start.32) | collective-permute-done | bytes 131104 | tf_op jit(solution)/shard_map/ppermute | solution.py:30
  177.2 1.1 shard_map.78
  178.6 1.1 shard_map.79
  179.7 1.9 collective-permute-start.34
  181.7 1.9 collective-permute-done.34.db
  183.5 2.3 %shard_map.82 = bf16[16,32,1024]{2,1,0:T(8,128)(2,1)} custom-call(s32[13]{0:T(128)S(1)} %concatenate.3.flags, bf16[512,256]{1,0:T(8,128)(2,1)S(1)} %get-tuple-element.167.za, bf16[512,256]{1,0:T(8,128)(2,1)S(1)} %collective-permute-done.12.zb, bf16[2,128,1024]{2,1,0:T(8,128)(2,1)S(1)} %get-tuple-element.169.da, ...), custom_call_target="tpu_custom_call" | custom-call | tf_op jit(solution)/shard_map/pallas_call | solution.py:34
  185.8 3.7 %all-to-all-start = ((bf16[16,32,1024]{2,1,0:T(8,128)(2,1)}), bf16[16,32,1024]{2,1,0:T(8,128)(2,1)S(1)}, u32[]{:S(2)}, u32[]{:S(2)}) async-start(bf16[16,32,1024]{2,1,0:T(8,128)(2,1)} %shard_map.82), calls=%async_computation | async-start | bytes 2097152 | tf_op jit(solution)/shard_map/all_to_all | solution.py:311
  190.2 17.6 %all-to-all-done.parts = bf16[16,32,1024]{2,1,0:T(8,128)(2,1)S(1)} async-done(((bf16[16,32,1024]{2,1,0:T(8,128)(2,1)}), bf16[16,32,1024]{2,1,0:T(8,128)(2,1)S(1)}, u32[]{:S(2)}, u32[]{:S(2)}) %all-to-all-start) | async-done | bytes 1048608 | tf_op jit(solution)/shard_map/all_to_all | solution.py:311
  208.5 7.3 %collective-permute-start.35 = (f32[16,1024]{1,0:T(8,128)S(1)}, f32[16,1024]{1,0:T(8,128)S(1)}, u32[]{:S(2)}, u32[]{:S(2)}) collective-permute-start(f32[16,1024]{1,0:T(8,128)S(1)} %get-tuple-element.171), channel_id=1, source_target_pairs={{0,8},{1,9},{2,10},{3,11},{4,12},{5,13},{6,14},{7,15},{8,0},{9,1},... | collective-permute-start | bytes 196616 | tf_op jit(solution)/shard_map/ppermute | solution.py:30
  217.2 5.0 %collective-permute-done.35.b = f32[16,1024]{1,0:T(8,128)S(1)} collective-permute-done((f32[16,1024]{1,0:T(8,128)S(1)}, f32[16,1024]{1,0:T(8,128)S(1)}, u32[]{:S(2)}, u32[]{:S(2)}) %collective-permute-start.35) | collective-permute-done | bytes 65568 | tf_op jit(solution)/shard_map/ppermute | solution.py:30
  (93 shorter events, 33.1 us)
Async XLA Ops:
  4.6 4.2 %collective-permute-start = (bf16[336,1024]{1,0:T(8,128)(2,1)S(1)}, bf16[336,1024]{1,0:T(8,128)(2,1)S(1)}, u32[]{:S(2)}, u32[]{:S(2)}) collective-permute-start(bf16[336,1024]{1,0:T(8,128)(2,1)S(1)} %get-tuple-element.87), channel_id=1, source_target_pairs={{448,449},{449,448},{450,451},{451,450},{452,453},{453,452},{454,4... | collective-permute-start | bytes 2064392 | tf_op jit(solution)/shard_map/ppermute | solution.py:30
  5.3 3.5 %collective-permute-start.1 = (bf16[336,1024]{1,0:T(8,128)(2,1)S(1)}, bf16[336,1024]{1,0:T(8,128)(2,1)S(1)}, u32[]{:S(2)}, u32[]{:S(2)}) collective-permute-start(bf16[336,1024]{1,0:T(8,128)(2,1)S(1)} %get-tuple-element.88), channel_id=1, source_target_pairs={{448,511},{449,450},{450,449},{451,452},{452,451},{453,454},{454,4... | collective-permute-start | bytes 2064392 | tf_op jit(solution)/shard_map/ppermute | solution.py:30
  11.1 12.7 %collective-permute-start.4 = (bf16[208,1024]{1,0:T(8,128)(2,1)S(1)}, bf16[208,1024]{1,0:T(8,128)(2,1)S(1)}, u32[]{:S(2)}, u32[]{:S(2)}) collective-permute-start(bf16[208,1024]{1,0:T(8,128)(2,1)S(1)} %get-tuple-element.100), channel_id=1, source_target_pairs={{0,1},{1,0},{2,3},{3,2},{4,5},{5,4},{6,7},{7,6},{8,9},{9,8},{10,11... | collective-permute-start | bytes 1277960 | tf_op jit(solution)/shard_map/ppermute | solution.py:30
  19.8 9.4 %collective-permute-start.5 = (bf16[208,1024]{1,0:T(8,128)(2,1)S(1)}, bf16[208,1024]{1,0:T(8,128)(2,1)S(1)}, u32[]{:S(2)}, u32[]{:S(2)}) collective-permute-start(bf16[208,1024]{1,0:T(8,128)(2,1)S(1)} %get-tuple-element.101), channel_id=1, source_target_pairs={{0,63},{1,2},{2,1},{3,4},{4,3},{5,6},{6,5},{7,8},{8,7},{9,10},{10,... | collective-permute-start | bytes 1277960 | tf_op jit(solution)/shard_map/ppermute | solution.py:30
  21.7 10.6 %collective-permute-start.6 = (bf16[128,1024]{1,0:T(8,128)(2,1)S(1)}, bf16[128,1024]{1,0:T(8,128)(2,1)S(1)}, u32[]{:S(2)}, u32[]{:S(2)}) collective-permute-start(bf16[128,1024]{1,0:T(8,128)(2,1)S(1)} %get-tuple-element.107), channel_id=1, source_target_pairs={{448,384},{449,385},{450,386},{451,387},{452,388},{453,389},{454,3... | collective-permute-start | bytes 786440 | tf_op jit(solution)/shard_map/ppermute | solution.py:30
  22.4 10.5 %collective-permute-start.2 = (bf16[128,1024]{1,0:T(8,128)(2,1)S(1)}, bf16[128,1024]{1,0:T(8,128)(2,1)S(1)}, u32[]{:S(2)}, u32[]{:S(2)}) collective-permute-start(bf16[128,1024]{1,0:T(8,128)(2,1)S(1)} %get-tuple-element.94), channel_id=1, source_target_pairs={{448,384},{449,385},{450,386},{451,387},{452,388},{453,389},{454,3... | collective-permute-start | bytes 786440 | tf_op jit(solution)/shard_map/ppermute | solution.py:30
  23.1 9.2 %collective-permute-start.7 = (bf16[64,1024]{1,0:T(8,128)(2,1)S(1)}, bf16[64,1024]{1,0:T(8,128)(2,1)S(1)}, u32[]{:S(2)}, u32[]{:S(2)}) collective-permute-start(bf16[64,1024]{1,0:T(8,128)(2,1)S(1)} %get-tuple-element.108), channel_id=1, source_target_pairs={{448,385},{449,386},{450,387},{451,388},{452,389},{453,390},{454,3... | collective-permute-start | bytes 393224 | tf_op jit(solution)/shard_map/ppermute | solution.py:30
  23.8 9.1 %collective-permute-start.3 = (bf16[64,1024]{1,0:T(8,128)(2,1)S(1)}, bf16[64,1024]{1,0:T(8,128)(2,1)S(1)}, u32[]{:S(2)}, u32[]{:S(2)}) collective-permute-start(bf16[64,1024]{1,0:T(8,128)(2,1)S(1)} %get-tuple-element.95), channel_id=1, source_target_pairs={{448,385},{449,386},{450,387},{451,388},{452,389},{453,390},{454,3... | collective-permute-start | bytes 393224 | tf_op jit(solution)/shard_map/ppermute | solution.py:30
  34.2 28.9 %collective-permute-start.12 = (bf16[512,256]{1,0:T(8,128)(2,1)S(1)}, bf16[512,256]{1,0:T(8,128)(2,1)S(1)}, u32[]{:S(2)}, u32[]{:S(2)}) collective-permute-start(bf16[512,256]{1,0:T(8,128)(2,1)S(1)} %get-tuple-element.121), channel_id=1, source_target_pairs={{0,1},{1,0},{2,3},{3,2},{4,5},{5,4},{6,7},{7,6},{8,9},{9,8},{10,11... | collective-permute-start | bytes 786440 | tf_op jit(solution)/shard_map/ppermute | solution.py:30
  61.1 3.3 %collective-permute-start.8 = (bf16[128,1024]{1,0:T(8,128)(2,1)S(1)}, bf16[128,1024]{1,0:T(8,128)(2,1)S(1)}, u32[]{:S(2)}, u32[]{:S(2)}) collective-permute-start(bf16[128,1024]{1,0:T(8,128)(2,1)S(1)} %get-tuple-element.113), channel_id=1, source_target_pairs={{384,320},{385,321},{386,322},{387,323},{388,324},{389,325},{390,3... | collective-permute-start | bytes 786440 | tf_op jit(solution)/shard_map/ppermute | solution.py:30
  63.7 3.3 %collective-permute-start.15 = (bf16[128,1024]{1,0:T(8,128)(2,1)S(1)}, bf16[128,1024]{1,0:T(8,128)(2,1)S(1)}, u32[]{:S(2)}, u32[]{:S(2)}) collective-permute-start(bf16[128,1024]{1,0:T(8,128)(2,1)S(1)} %get-tuple-element.128), channel_id=1, source_target_pairs={{320,256},{321,257},{322,258},{323,259},{324,260},{325,261},{326,2... | collective-permute-start | bytes 786440 | tf_op jit(solution)/shard_map/ppermute | solution.py:30
  65.0 3.3 %collective-permute-start.13 = (bf16[128,1024]{1,0:T(8,128)(2,1)S(1)}, bf16[128,1024]{1,0:T(8,128)(2,1)S(1)}, u32[]{:S(2)}, u32[]{:S(2)}) collective-permute-start(bf16[128,1024]{1,0:T(8,128)(2,1)S(1)} %get-tuple-element.126), channel_id=1, source_target_pairs={{320,256},{321,257},{322,258},{323,259},{324,260},{325,261},{326,2... | collective-permute-start | bytes 786440 | tf_op jit(solution)/shard_map/ppermute | solution.py:30
  68.9 3.3 %collective-permute-start.17 = (bf16[128,1024]{1,0:T(8,128)(2,1)S(1)}, bf16[128,1024]{1,0:T(8,128)(2,1)S(1)}, u32[]{:S(2)}, u32[]{:S(2)}) collective-permute-start(bf16[128,1024]{1,0:T(8,128)(2,1)S(1)} %get-tuple-element.134), channel_id=1, source_target_pairs={{256,192},{257,193},{258,194},{259,195},{260,196},{261,197},{262,1... | collective-permute-start | bytes 786440 | tf_op jit(solution)/shard_map/ppermute | solution.py:30
  71.5 3.5 %collective-permute-start.23 = (bf16[128,1024]{1,0:T(8,128)(2,1)S(1)}, bf16[128,1024]{1,0:T(8,128)(2,1)S(1)}, u32[]{:S(2)}, u32[]{:S(2)}) collective-permute-start(bf16[128,1024]{1,0:T(8,128)(2,1)S(1)} %get-tuple-element.144), channel_id=1, source_target_pairs={{192,128},{193,129},{194,130},{195,131},{196,132},{197,133},{198,1... | collective-permute-start | bytes 786440 | tf_op jit(solution)/shard_map/ppermute | solution.py:30
  73.0 3.3 %collective-permute-start.21 = (bf16[128,1024]{1,0:T(8,128)(2,1)S(1)}, bf16[128,1024]{1,0:T(8,128)(2,1)S(1)}, u32[]{:S(2)}, u32[]{:S(2)}) collective-permute-start(bf16[128,1024]{1,0:T(8,128)(2,1)S(1)} %get-tuple-element.142), channel_id=1, source_target_pairs={{192,128},{193,129},{194,130},{195,131},{196,132},{197,133},{198,1... | collective-permute-start | bytes 786440 | tf_op jit(solution)/shard_map/ppermute | solution.py:30
  76.8 3.9 %collective-permute-start.25 = (bf16[128,1024]{1,0:T(8,128)(2,1)S(1)}, bf16[128,1024]{1,0:T(8,128)(2,1)S(1)}, u32[]{:S(2)}, u32[]{:S(2)}) collective-permute-start(bf16[128,1024]{1,0:T(8,128)(2,1)S(1)} %get-tuple-element.150), channel_id=1, source_target_pairs={{128,64},{129,65},{130,66},{131,67},{132,68},{133,69},{134,70},{13... | collective-permute-start | bytes 786440 | tf_op jit(solution)/shard_map/ppermute | solution.py:30
  79.5 97.7 %collective-permute-start.31 = (bf16[128,1024]{1,0:T(8,128)(2,1)S(1)}, bf16[128,1024]{1,0:T(8,128)(2,1)S(1)}, u32[]{:S(2)}, u32[]{:S(2)}) collective-permute-start(bf16[128,1024]{1,0:T(8,128)(2,1)S(1)} %get-tuple-element.160), channel_id=1, source_target_pairs={{64,0},{65,1},{66,2},{67,3},{68,4},{69,5},{70,6},{71,7},{72,8},{73... | collective-permute-start | bytes 786440 | tf_op jit(solution)/shard_map/ppermute | solution.py:30
  81.3 97.3 %collective-permute-start.29 = (bf16[128,1024]{1,0:T(8,128)(2,1)S(1)}, bf16[128,1024]{1,0:T(8,128)(2,1)S(1)}, u32[]{:S(2)}, u32[]{:S(2)}) collective-permute-start(bf16[128,1024]{1,0:T(8,128)(2,1)S(1)} %get-tuple-element.158), channel_id=1, source_target_pairs={{64,0},{65,1},{66,2},{67,3},{68,4},{69,5},{70,6},{71,7},{72,8},{73... | collective-permute-start | bytes 786440 | tf_op jit(solution)/shard_map/ppermute | solution.py:30
  82.6 94.6 %collective-permute-start.32 = (bf16[64,1024]{1,0:T(8,128)(2,1)S(1)}, bf16[64,1024]{1,0:T(8,128)(2,1)S(1)}, u32[]{:S(2)}, u32[]{:S(2)}) collective-permute-start(bf16[64,1024]{1,0:T(8,128)(2,1)S(1)} %get-tuple-element.161), channel_id=1, source_target_pairs={{64,1},{65,2},{66,3},{67,4},{68,5},{69,6},{70,7},{71,8},{72,9},{73... | collective-permute-start | bytes 393224 | tf_op jit(solution)/shard_map/ppermute | solution.py:30
  83.9 94.7 %collective-permute-start.30 = (bf16[64,1024]{1,0:T(8,128)(2,1)S(1)}, bf16[64,1024]{1,0:T(8,128)(2,1)S(1)}, u32[]{:S(2)}, u32[]{:S(2)}) collective-permute-start(bf16[64,1024]{1,0:T(8,128)(2,1)S(1)} %get-tuple-element.159), channel_id=1, source_target_pairs={{64,1},{65,2},{66,3},{67,4},{68,5},{69,6},{70,7},{71,8},{72,9},{73... | collective-permute-start | bytes 393224 | tf_op jit(solution)/shard_map/ppermute | solution.py:30
  179.7 3.8 %collective-permute-start.34 = (bf16[2,128,1024]{2,1,0:T(8,128)(2,1)S(1)}, bf16[2,128,1024]{2,1,0:T(8,128)(2,1)S(1)}, u32[]{:S(2)}, u32[]{:S(2)}) collective-permute-start(bf16[2,128,1024]{2,1,0:T(8,128)(2,1)S(1)} %get-tuple-element.169.da), channel_id=1, source_target_pairs={{0,1},{1,0},{2,3},{3,2},{4,5},{5,4},{6,7},{7,6},{8,9},{9,8},{10,11... | collective-permute-start | bytes 1572872 | tf_op jit(solution)/shard_map/ppermute | solution.py:30
  185.8 21.9 %all-to-all-start = ((bf16[16,32,1024]{2,1,0:T(8,128)(2,1)}), bf16[16,32,1024]{2,1,0:T(8,128)(2,1)S(1)}, u32[]{:S(2)}, u32[]{:S(2)}) async-start(bf16[16,32,1024]{2,1,0:T(8,128)(2,1)} %shard_map.82), calls=%async_computation | async-start | bytes 2097152 | tf_op jit(solution)/shard_map/all_to_all | solution.py:311
  189.5 26.3 %collective-permute-start.33 = (bf16[2,32,1024]{2,1,0:T(8,128)(2,1)S(1)}, bf16[2,32,1024]{2,1,0:T(8,128)(2,1)S(1)}, u32[]{:S(2)}, u32[]{:S(2)}) collective-permute-start(bf16[2,32,1024]{2,1,0:T(8,128)(2,1)S(1)} %shard_map.80), channel_id=1, source_target_pairs={{64,65},{65,66},{66,67},{67,68},{68,69},{69,70},{70,71},{71,72},{7... | collective-permute-start | bytes 393224 | tf_op jit(solution)/shard_map/ppermute | solution.py:30
  208.5 13.7 %collective-permute-start.35 = (f32[16,1024]{1,0:T(8,128)S(1)}, f32[16,1024]{1,0:T(8,128)S(1)}, u32[]{:S(2)}, u32[]{:S(2)}) collective-permute-start(f32[16,1024]{1,0:T(8,128)S(1)} %get-tuple-element.171), channel_id=1, source_target_pairs={{0,8},{1,9},{2,10},{3,11},{4,12},{5,13},{6,14},{7,15},{8,0},{9,1},... | collective-permute-start | bytes 196616 | tf_op jit(solution)/shard_map/ppermute | solution.py:30
  (19 other events, 34.7 us)

commit v3 on v2

--- a/solution.py
+++ b/solution.py
@@ -45,8 +45,15 @@
     out[...] = w[...].T
 
 
-def pack_kernel(flags, h, up, neighbours, off, *edges):
+def pack_kernel(flags, h_ref, up_ref, neighbours, off, *rest):
+    *edges, h, up, sems = rest
     micro, rows, width = h.shape
+    copies = [
+        pltpu.make_async_copy(h_ref, h, sems.at[0]),
+        pltpu.make_async_copy(up_ref, up, sems.at[1]),
+    ]
+    for copy in copies:
+        copy.start()
     nodes = flags[NODES]
     even = flags[EVEN] == 1
     ids = flags[BASE] + lax.broadcasted_iota(jnp.int32, neighbours.shape, 0)
@@ -55,6 +62,8 @@
     step = jnp.where(step < -HALO, step + nodes, step)
     off[...] = jnp.zeros(off.shape, bf16)
     off[:, :K] = step.astype(f32).astype(bf16)
+    for copy in copies:
+        copy.wait()
     blank = jnp.zeros((16, width - 512), bf16)
 
     def edge(upper):
@@ -68,9 +77,9 @@
 
     lower, upper = edge(False), edge(True)
     x, y = jnp.where(even, upper, lower), jnp.where(even, lower, upper)
-    for value, full, short in ((x, edges[0], edges[2]), (y, edges[1], edges[3])):
-        full[...] = value
-        short[...] = value[: short.shape[0]]
+    edges[0][...] = x
+    edges[1][...] = y
+    edges[2][...] = y[: edges[2].shape[0]]
 
 
 def slope(u):
@@ -173,30 +182,33 @@
         other[16 * q : 16 * q + 16, :] = jnp.where(even, b, a)
 
 
-def weight_kernel(flags, za, zb, da, db, out):
+def weight_kernel(flags, za, zb, da, db, far, near):
     micro, rows, width = da.shape
     total = jnp.dot(za[...], da[...].reshape(micro * rows, width), preferred_element_type=f32)
     total = total + jnp.dot(
         zb[...], db[...].reshape(micro * rows, width), preferred_element_type=f32
     )
     total = total.astype(bf16)
-    for q in range(2 * out.shape[0]):
-        y, z_hi, x = q // 8, (q // 4) % 2, q % 4
-        out[4 * y + x, 16 * z_hi : 16 * z_hi + 16, :] = total[16 * q : 16 * q + 16]
-
-
-def sum_kernel(flags, parts, mine, other):
+    upper = flags[LOWER] == 1
+    for y in range(4):
+        for x in range(4):
+            a, b = (total[16 * q : 16 * q + 16] for q in (8 * y + x, 8 * y + 4 + x))
+            far[4 * y + x] = jnp.where(upper, a, b)
+            near[4 * y + x] = jnp.where(upper, b, a)
+
+
+def sum_kernel(flags, parts, out):
     total = parts[0].astype(f32)
     for i in range(1, parts.shape[0]):
         total = total + parts[i].astype(f32)
-    first = flags[LOWER] == 0
-    a, b = total[:16], total[16:]
-    mine[...] = jnp.where(first, a, b)
-    other[...] = jnp.where(first, b, a)
-
-
-def add_kernel(flags, a, b, out):
-    out[...] = a[...] + b[...]
+    out[...] = total
+
+
+def add_kernel(flags, parts, other, out):
+    total = parts[0].astype(f32)
+    for i in range(1, parts.shape[0]):
+        total = total + parts[i].astype(f32)
+    out[...] = total + other[...]
 
 
 def shards(acts, upstream, weights, neighbours):
@@ -235,14 +247,24 @@
 
     short = ((micro * WIDE + 16, width), bf16)
     long = ((micro * (WIDE + EDGE) + 16, width), bf16)
-    off, tx, ty, x_pack, y_pack = call(
+    shapes = [((rows, 128), bf16), long, long, short]
+    whole = pl.BlockSpec(memory_space=pltpu.HBM)
+    off, from_x, ty, y_pack = pl.pallas_call(
         pack_kernel,
-        [((rows, 128), bf16), long, long, short, short],
-        flags,
-        [h, upstream, neighbours],
-    )
+        out_shape=tuple(pltpu.VMEM(shape, dtype) for shape, dtype in shapes),
+        in_specs=[SMEM, whole, whole, VMEM],
+        out_specs=tuple([VMEM] * len(shapes)),
+        scratch_shapes=[
+            pltpu.VMEM((micro, rows, width), bf16),
+            pltpu.VMEM((micro, rows, width), bf16),
+            pltpu.SemaphoreType.DMA((2,)),
+        ],
+        compiler_params=LIMIT,
+        name="pack",
+    )(flags, *(pltpu.with_memory_space_constraint(a, pltpu.HBM) for a in (h, upstream)), on_chip(neighbours))
+    h, upstream, off = lax.optimization_barrier((h, upstream, off))
     ty = permute(ty, edges(1, top, 0))
-    tx = permute(tx, edges(0, top, 0))
+    from_x = permute(from_x, swap(1))
     (w_t,) = call(turn_kernel, [((width, width), bf16)], flags, [w])
     field = ((micro, rows, width), bf16)
     made = [((micro, span, width), f32), ((reach, span), bf16), field]
@@ -256,17 +278,14 @@
             {6 + i: i for i in range(len(old))},
         )
 
-    prepared = prepare(top[0], (tx, ty))
+    prepared = prepare(top[0], (from_x, ty))
     grads = kept = None
-    received = [[upstream, tx, ty]] * micro
+    received = [[upstream, from_x, ty]] * micro
     for layer in reversed(range(sections)):
         if layer == rest[-1]:
-            x_pack, y_pack, grads, *prepared = lax.optimization_barrier(
-                (x_pack, y_pack, grads, *prepared)
-            )
+            y_pack, grads, *prepared = lax.optimization_barrier((y_pack, grads, *prepared))
             ry = permute(y_pack, edges(1, rest, 0))
-            rx = permute(x_pack, edges(0, rest, 0))
-            prepared = prepare(REST, (rx, ry), prepared)
+            prepared = prepare(REST, (from_x, ry), prepared)
         if layer == rest[-1] - 1:
             half_shape = ((width // 2, micro * rows), bf16)
             grads, z = lax.optimization_barrier((grads, prepared[2]))
@@ -297,22 +316,20 @@
             rim = permute(rim, toward(range(1, sections, 2), 0, 1))
 
     du_other = permute(kept, swap(1))
-    (partial,) = call(
-        weight_kernel,
-        [((count // 4, 2 * width // count, width), bf16)],
-        flags,
-        [mine, other, kept, du_other],
+    slab = (width // count, width)
+    far, close = call(
+        weight_kernel, [((16, *slab), bf16)] * 2, flags, [mine, other, kept, du_other]
     )
     groups = [
         [16 * y + 8 * z + 2 * x + c for y in range(4) for x in range(4)]
         for z in range(2)
         for c in range(2)
     ]
-    parts = lax.all_to_all(partial, "space", 0, 0, axis_index_groups=groups)
-    slab = ((width // count, width), f32)
-    mine, other = call(sum_kernel, [slab, slab], flags, [parts])
-    other = permute(other, swap(8))
-    (weight_grad,) = call(add_kernel, [slab], flags, [mine, other])
+    far = lax.all_to_all(far, "space", 0, 0, axis_index_groups=groups)
+    close = lax.all_to_all(close, "space", 0, 0, axis_index_groups=groups)
+    (far,) = call(sum_kernel, [(slab, f32)], flags, [far])
+    other = permute(far, swap(8))
+    (weight_grad,) = call(add_kernel, [(slab, f32)], flags, [close, other])
     (grads,) = call(shift_kernel, [field], flags, [grads, rim])
     return (grads[None], weight_grad[None])
 

time: 224 us -> 225 us (level)
  the two profiles are of different devices: /device:TPU:1 before, /device:TPU:47 now
where the time goes in v3:
time: 225 us; the launch traced here: 224 us
  waiting for transfers between devices  95 us (42%)
  starting transfers between devices  76.1 us (34%)
  blocking collectives  25.2 us (11%)
  Pallas kernels  22.1 us (10%)
  local copies, waits for them, and re-layouts  4.49 us (2%)
    ppermute x35, waiting for transfers between devices, permute(): return lax.ppermute(value, AXES, pairs)  95 us
    ppermute x35, starting transfers between devices, permute(): return lax.ppermute(value, AXES, pairs)  69 us
    all_to_all x1, blocking collectives, shards(): far = lax.all_to_all(far, 'space', 0, 0, axis_index_groups=groups)  25.2 us
    pallas_call x25, Pallas kernels, call(): pl.pallas_call(kernel, out_shape=tuple((pltpu.VMEM(shape, dtype) for shap...  20.1 us
    all_to_all x1, starting transfers between devices, shards(): close = lax.all_to_all(close, 'space', 0, 0, axis_index_groups=groups)  7.06 us
  transfers between devices with their start and end apart: 36, of which 6 were waited for; matrix products, arithmetic and copies ran while one was open for 0% of the time, Pallas kernels for 6%

profile of v3, /device:TPU:47, one launch (start us, length us, event | category | flops | bytes accessed | tf_op | source)
XLA Modules:
  0.0 224.3 jit_solution(16903020247959260317)
XLA Ops:
  1.6 1.9 pack.1
  3.5 2.6 %collective-permute-start = (bf16[336,1024]{1,0:T(8,128)(2,1)S(1)}, bf16[336,1024]{1,0:T(8,128)(2,1)S(1)}, u32[]{:S(2)}, u32[]{:S(2)}) collective-permute-start(bf16[336,1024]{1,0:T(8,128)(2,1)S(1)} %get-tuple-element.90), channel_id=1, source_target_pairs={{0,1},{1,0},{2,3},{3,2},{4,5},{5,4},{6,7},{7,6},{8,9},{9,8},{10,11... | collective-permute-start | bytes 2064392 | tf_op jit(solution)/shard_map/ppermute | solution.py:30
  6.8 1.6 copy-done
  11.9 14.4 %collective-permute-start.4 = (bf16[208,1024]{1,0:T(8,128)(2,1)S(1)}, bf16[208,1024]{1,0:T(8,128)(2,1)S(1)}, u32[]{:S(2)}, u32[]{:S(2)}) collective-permute-start(bf16[208,1024]{1,0:T(8,128)(2,1)S(1)} %get-tuple-element.103), channel_id=1, source_target_pairs={{0,63},{1,2},{2,1},{3,4},{4,3},{5,6},{6,5},{7,8},{8,7},{9,10},{10,... | collective-permute-start | bytes 1277960 | tf_op jit(solution)/shard_map/ppermute | solution.py:30
  29.0 19.9 %collective-permute-done.4.from_y = bf16[208,1024]{1,0:T(8,128)(2,1)S(1)} collective-permute-done((bf16[208,1024]{1,0:T(8,128)(2,1)S(1)}, bf16[208,1024]{1,0:T(8,128)(2,1)S(1)}, u32[]{:S(2)}, u32[]{:S(2)}) %collective-permute-start.4) | collective-permute-done | bytes 426016 | tf_op jit(solution)/shard_map/ppermute | solution.py:30
  48.9 3.1 %shard_map.63 = (f32[2,256,1024]{2,1,0:T(8,128)S(1)}, bf16[320,256]{1,0:T(8,128)(2,1)S(1)}, bf16[2,128,1024]{2,1,0:T(8,128)(2,1)S(1)}) custom-call(s32[13]{0:T(128)S(1)} %concatenate.3.flags, bf16[2,128,1024]{2,1,0:T(8,128)(2,1)S(1)} %bitcast.15, ...), custom_call_target="tpu_custom_call", output_to_operand_aliasing={{0}: (6, {}), {1}: (7, {}), {2}: (8, {})} | custom-call | tf_op jit(solution)/shard_map/pallas_call | solution.py:34
  53.9 1.9 collective-permute-start.11
  70.9 1.3 collective-permute-start.26
  72.8 1.3 collective-permute-start.24
  74.1 1.3 collective-permute-start.27
  76.7 65.1 %collective-permute-done.27.refs_1_ = bf16[64,1024]{1,0:T(8,128)(2,1)S(1)} collective-permute-done((bf16[64,1024]{1,0:T(8,128)(2,1)S(1)}, bf16[64,1024]{1,0:T(8,128)(2,1)S(1)}, u32[]{:S(2)}, u32[]{:S(2)}) %collective-permute-start.27) | collective-permute-done | bytes 131104 | tf_op jit(solution)/shard_map/ppermute | solution.py:30
  142.9 1.3 collective-permute-start.30
  145.4 1.3 collective-permute-start.28
  146.7 1.3 collective-permute-start.31
  148.0 1.3 collective-permute-start.29
  150.5 1.5 collective-permute-done.29.refs_1_
  152.6 9.0 %collective-permute-start.33 = (bf16[2,128,1024]{2,1,0:T(8,128)(2,1)S(1)}, bf16[2,128,1024]{2,1,0:T(8,128)(2,1)S(1)}, u32[]{:S(2)}, u32[]{:S(2)}) collective-permute-start(bf16[2,128,1024]{2,1,0:T(8,128)(2,1)S(1)} %get-tuple-element.171.da), channel_id=1, source_target_pairs={{0,1},{1,0},{2,3},{3,2},{4,5},{5,4},{6,7},{7,6},{8,9},{9,8},{10,11... | collective-permute-start | bytes 1572872 | tf_op jit(solution)/shard_map/ppermute | solution.py:30
  161.6 1.5 collective-permute-done.33.db
  163.1 2.1 shard_map.81
  165.2 25.2 %all_to_all.10.parts = bf16[16,16,1024]{2,1,0:T(8,128)(2,1)S(1)} all-to-all(bf16[16,16,1024]{2,1,0:T(8,128)(2,1)S(1)} %get-tuple-element.173), channel_id=1, replica_groups={{0,2,4,6,16,18,20,22,32,34,36,38,48,50,52,54},{1,3,5,7,17,19,21,23,33,3..., dimensions={0} | all-to-all | bytes 1048576 | tf_op jit(solution)/shard_map/all_to_all | solution.py:328
  190.4 7.1 %all-to-all-start = ((bf16[16,16,1024]{2,1,0:T(8,128)(2,1)}), bf16[16,16,1024]{2,1,0:T(8,128)(2,1)S(1)}, u32[]{:S(2)}, u32[]{:S(2)}) async-start(bf16[16,16,1024]{2,1,0:T(8,128)(2,1)} %get-tuple-element.172), calls=%async_computation | async-start | bytes 1048576 | tf_op jit(solution)/shard_map/all_to_all | solution.py:329
  197.5 11.2 %collective-permute-start.32 = (bf16[2,32,1024]{2,1,0:T(8,128)(2,1)S(1)}, bf16[2,32,1024]{2,1,0:T(8,128)(2,1)S(1)}, u32[]{:S(2)}, u32[]{:S(2)}) collective-permute-start(bf16[2,32,1024]{2,1,0:T(8,128)(2,1)S(1)} %shard_map.79), channel_id=1, source_target_pairs={{64,65},{65,66},{66,67},{67,68},{68,69},{69,70},{70,71},{71,72},{7... | collective-permute-start | bytes 393224 | tf_op jit(solution)/shard_map/ppermute | solution.py:30
  209.3 5.4 %collective-permute-start.34 = (f32[16,1024]{1,0:T(8,128)S(1)}, f32[16,1024]{1,0:T(8,128)S(1)}, u32[]{:S(2)}, u32[]{:S(2)}) collective-permute-start(f32[16,1024]{1,0:T(8,128)S(1)} %shard_map.82), channel_id=1, source_target_pairs={{0,8},{1,9},{2,10},{3,11},{4,12},{5,13},{6,14},{7,15},{8,0},{9,1},... | collective-permute-start | bytes 196616 | tf_op jit(solution)/shard_map/ppermute | solution.py:30
  216.1 6.9 %collective-permute-done.34.other = f32[16,1024]{1,0:T(8,128)S(1)} collective-permute-done((f32[16,1024]{1,0:T(8,128)S(1)}, f32[16,1024]{1,0:T(8,128)S(1)}, u32[]{:S(2)}, u32[]{:S(2)}) %collective-permute-start.34) | collective-permute-done | bytes 65568 | tf_op jit(solution)/shard_map/ppermute | solution.py:30
  (88 shorter events, 33.5 us)
Async XLA Ops:
  3.5 6.1 %collective-permute-start = (bf16[336,1024]{1,0:T(8,128)(2,1)S(1)}, bf16[336,1024]{1,0:T(8,128)(2,1)S(1)}, u32[]{:S(2)}, u32[]{:S(2)}) collective-permute-start(bf16[336,1024]{1,0:T(8,128)(2,1)S(1)} %get-tuple-element.90), channel_id=1, source_target_pairs={{0,1},{1,0},{2,3},{3,2},{4,5},{5,4},{6,7},{7,6},{8,9},{9,8},{10,11... | collective-permute-start | bytes 2064392 | tf_op jit(solution)/shard_map/ppermute | solution.py:30
  6.1 3.5 %collective-permute-start.1 = (bf16[336,1024]{1,0:T(8,128)(2,1)S(1)}, bf16[336,1024]{1,0:T(8,128)(2,1)S(1)}, u32[]{:S(2)}, u32[]{:S(2)}) collective-permute-start(bf16[336,1024]{1,0:T(8,128)(2,1)S(1)} %get-tuple-element.91), channel_id=1, source_target_pairs={{448,511},{449,450},{450,449},{451,452},{452,451},{453,454},{454,4... | collective-permute-start | bytes 2064392 | tf_op jit(solution)/shard_map/ppermute | solution.py:30
  11.9 37.0 %collective-permute-start.4 = (bf16[208,1024]{1,0:T(8,128)(2,1)S(1)}, bf16[208,1024]{1,0:T(8,128)(2,1)S(1)}, u32[]{:S(2)}, u32[]{:S(2)}) collective-permute-start(bf16[208,1024]{1,0:T(8,128)(2,1)S(1)} %get-tuple-element.103), channel_id=1, source_target_pairs={{0,63},{1,2},{2,1},{3,4},{4,3},{5,6},{6,5},{7,8},{8,7},{9,10},{10,... | collective-permute-start | bytes 1277960 | tf_op jit(solution)/shard_map/ppermute | solution.py:30
  26.3 25.7 %collective-permute-start.5 = (bf16[128,1024]{1,0:T(8,128)(2,1)S(1)}, bf16[128,1024]{1,0:T(8,128)(2,1)S(1)}, u32[]{:S(2)}, u32[]{:S(2)}) collective-permute-start(bf16[128,1024]{1,0:T(8,128)(2,1)S(1)} %get-tuple-element.109), channel_id=1, source_target_pairs={{448,384},{449,385},{450,386},{451,387},{452,388},{453,389},{454,3... | collective-permute-start | bytes 786440 | tf_op jit(solution)/shard_map/ppermute | solution.py:30
  27.0 25.6 %collective-permute-start.2 = (bf16[128,1024]{1,0:T(8,128)(2,1)S(1)}, bf16[128,1024]{1,0:T(8,128)(2,1)S(1)}, u32[]{:S(2)}, u32[]{:S(2)}) collective-permute-start(bf16[128,1024]{1,0:T(8,128)(2,1)S(1)} %get-tuple-element.98), channel_id=1, source_target_pairs={{448,384},{449,385},{450,386},{451,387},{452,388},{453,389},{454,3... | collective-permute-start | bytes 786440 | tf_op jit(solution)/shard_map/ppermute | solution.py:30
  27.6 24.3 %collective-permute-start.6 = (bf16[64,1024]{1,0:T(8,128)(2,1)S(1)}, bf16[64,1024]{1,0:T(8,128)(2,1)S(1)}, u32[]{:S(2)}, u32[]{:S(2)}) collective-permute-start(bf16[64,1024]{1,0:T(8,128)(2,1)S(1)} %get-tuple-element.110), channel_id=1, source_target_pairs={{448,385},{449,386},{450,387},{451,388},{452,389},{453,390},{454,3... | collective-permute-start | bytes 393224 | tf_op jit(solution)/shard_map/ppermute | solution.py:30
  28.3 24.2 %collective-permute-start.3 = (bf16[64,1024]{1,0:T(8,128)(2,1)S(1)}, bf16[64,1024]{1,0:T(8,128)(2,1)S(1)}, u32[]{:S(2)}, u32[]{:S(2)}) collective-permute-start(bf16[64,1024]{1,0:T(8,128)(2,1)S(1)} %get-tuple-element.99), channel_id=1, source_target_pairs={{448,385},{449,386},{450,387},{451,388},{452,389},{453,390},{454,3... | collective-permute-start | bytes 393224 | tf_op jit(solution)/shard_map/ppermute | solution.py:30
  53.9 4.7 %collective-permute-start.11 = (bf16[512,256]{1,0:T(8,128)(2,1)S(1)}, bf16[512,256]{1,0:T(8,128)(2,1)S(1)}, u32[]{:S(2)}, u32[]{:S(2)}) collective-permute-start(bf16[512,256]{1,0:T(8,128)(2,1)S(1)} %get-tuple-element.123), channel_id=1, source_target_pairs={{0,1},{1,0},{2,3},{3,2},{4,5},{5,4},{6,7},{7,6},{8,9},{9,8},{10,11... | collective-permute-start | bytes 786440 | tf_op jit(solution)/shard_map/ppermute | solution.py:30
  56.5 3.3 %collective-permute-start.7 = (bf16[128,1024]{1,0:T(8,128)(2,1)S(1)}, bf16[128,1024]{1,0:T(8,128)(2,1)S(1)}, u32[]{:S(2)}, u32[]{:S(2)}) collective-permute-start(bf16[128,1024]{1,0:T(8,128)(2,1)S(1)} %get-tuple-element.115), channel_id=1, source_target_pairs={{384,320},{385,321},{386,322},{387,323},{388,324},{389,325},{390,3... | collective-permute-start | bytes 786440 | tf_op jit(solution)/shard_map/ppermute | solution.py:30
  59.1 3.3 %collective-permute-start.14 = (bf16[128,1024]{1,0:T(8,128)(2,1)S(1)}, bf16[128,1024]{1,0:T(8,128)(2,1)S(1)}, u32[]{:S(2)}, u32[]{:S(2)}) collective-permute-start(bf16[128,1024]{1,0:T(8,128)(2,1)S(1)} %get-tuple-element.130), channel_id=1, source_target_pairs={{320,256},{321,257},{322,258},{323,259},{324,260},{325,261},{326,2... | collective-permute-start | bytes 786440 | tf_op jit(solution)/shard_map/ppermute | solution.py:30
  60.4 3.3 %collective-permute-start.12 = (bf16[128,1024]{1,0:T(8,128)(2,1)S(1)}, bf16[128,1024]{1,0:T(8,128)(2,1)S(1)}, u32[]{:S(2)}, u32[]{:S(2)}) collective-permute-start(bf16[128,1024]{1,0:T(8,128)(2,1)S(1)} %get-tuple-element.128), channel_id=1, source_target_pairs={{320,256},{321,257},{322,258},{323,259},{324,260},{325,261},{326,2... | collective-permute-start | bytes 786440 | tf_op jit(solution)/shard_map/ppermute | solution.py:30
  66.9 3.5 %collective-permute-start.22 = (bf16[128,1024]{1,0:T(8,128)(2,1)S(1)}, bf16[128,1024]{1,0:T(8,128)(2,1)S(1)}, u32[]{:S(2)}, u32[]{:S(2)}) collective-permute-start(bf16[128,1024]{1,0:T(8,128)(2,1)S(1)} %get-tuple-element.146), channel_id=1, source_target_pairs={{192,128},{193,129},{194,130},{195,131},{196,132},{197,133},{198,1... | collective-permute-start | bytes 786440 | tf_op jit(solution)/shard_map/ppermute | solution.py:30
  68.3 3.9 %collective-permute-start.20 = (bf16[128,1024]{1,0:T(8,128)(2,1)S(1)}, bf16[128,1024]{1,0:T(8,128)(2,1)S(1)}, u32[]{:S(2)}, u32[]{:S(2)}) collective-permute-start(bf16[128,1024]{1,0:T(8,128)(2,1)S(1)} %get-tuple-element.144), channel_id=1, source_target_pairs={{192,128},{193,129},{194,130},{195,131},{196,132},{197,133},{198,1... | collective-permute-start | bytes 786440 | tf_op jit(solution)/shard_map/ppermute | solution.py:30
  70.9 70.9 %collective-permute-start.26 = (bf16[128,1024]{1,0:T(8,128)(2,1)S(1)}, bf16[128,1024]{1,0:T(8,128)(2,1)S(1)}, u32[]{:S(2)}, u32[]{:S(2)}) collective-permute-start(bf16[128,1024]{1,0:T(8,128)(2,1)S(1)} %get-tuple-element.154), channel_id=1, source_target_pairs={{128,64},{129,65},{130,66},{131,67},{132,68},{133,69},{134,70},{13... | collective-permute-start | bytes 786440 | tf_op jit(solution)/shard_map/ppermute | solution.py:30
  72.8 71.4 %collective-permute-start.24 = (bf16[128,1024]{1,0:T(8,128)(2,1)S(1)}, bf16[128,1024]{1,0:T(8,128)(2,1)S(1)}, u32[]{:S(2)}, u32[]{:S(2)}) collective-permute-start(bf16[128,1024]{1,0:T(8,128)(2,1)S(1)} %get-tuple-element.152), channel_id=1, source_target_pairs={{128,64},{129,65},{130,66},{131,67},{132,68},{133,69},{134,70},{13... | collective-permute-start | bytes 786440 | tf_op jit(solution)/shard_map/ppermute | solution.py:30
  74.1 67.7 %collective-permute-start.27 = (bf16[64,1024]{1,0:T(8,128)(2,1)S(1)}, bf16[64,1024]{1,0:T(8,128)(2,1)S(1)}, u32[]{:S(2)}, u32[]{:S(2)}) collective-permute-start(bf16[64,1024]{1,0:T(8,128)(2,1)S(1)} %get-tuple-element.155), channel_id=1, source_target_pairs={{128,127},{129,64},{130,65},{131,66},{132,67},{133,68},{134,69},{1... | collective-permute-start | bytes 393224 | tf_op jit(solution)/shard_map/ppermute | solution.py:30
  75.4 68.8 %collective-permute-start.25 = (bf16[64,1024]{1,0:T(8,128)(2,1)S(1)}, bf16[64,1024]{1,0:T(8,128)(2,1)S(1)}, u32[]{:S(2)}, u32[]{:S(2)}) collective-permute-start(bf16[64,1024]{1,0:T(8,128)(2,1)S(1)} %get-tuple-element.153), channel_id=1, source_target_pairs={{128,127},{129,64},{130,65},{131,66},{132,67},{133,68},{134,69},{1... | collective-permute-start | bytes 393224 | tf_op jit(solution)/shard_map/ppermute | solution.py:30
  142.9 7.0 %collective-permute-start.30 = (bf16[128,1024]{1,0:T(8,128)(2,1)S(1)}, bf16[128,1024]{1,0:T(8,128)(2,1)S(1)}, u32[]{:S(2)}, u32[]{:S(2)}) collective-permute-start(bf16[128,1024]{1,0:T(8,128)(2,1)S(1)} %get-tuple-element.162), channel_id=1, source_target_pairs={{64,0},{65,1},{66,2},{67,3},{68,4},{69,5},{70,6},{71,7},{72,8},{73... | collective-permute-start | bytes 786440 | tf_op jit(solution)/shard_map/ppermute | solution.py:30
  145.4 6.6 %collective-permute-start.28 = (bf16[128,1024]{1,0:T(8,128)(2,1)S(1)}, bf16[128,1024]{1,0:T(8,128)(2,1)S(1)}, u32[]{:S(2)}, u32[]{:S(2)}) collective-permute-start(bf16[128,1024]{1,0:T(8,128)(2,1)S(1)} %get-tuple-element.160), channel_id=1, source_target_pairs={{64,0},{65,1},{66,2},{67,3},{68,4},{69,5},{70,6},{71,7},{72,8},{73... | collective-permute-start | bytes 786440 | tf_op jit(solution)/shard_map/ppermute | solution.py:30
  148.0 4.0 %collective-permute-start.29 = (bf16[64,1024]{1,0:T(8,128)(2,1)S(1)}, bf16[64,1024]{1,0:T(8,128)(2,1)S(1)}, u32[]{:S(2)}, u32[]{:S(2)}) collective-permute-start(bf16[64,1024]{1,0:T(8,128)(2,1)S(1)} %get-tuple-element.161), channel_id=1, source_target_pairs={{64,1},{65,2},{66,3},{67,4},{68,5},{69,6},{70,7},{71,8},{72,9},{73... | collective-permute-start | bytes 393224 | tf_op jit(solution)/shard_map/ppermute | solution.py:30
  152.6 10.6 %collective-permute-start.33 = (bf16[2,128,1024]{2,1,0:T(8,128)(2,1)S(1)}, bf16[2,128,1024]{2,1,0:T(8,128)(2,1)S(1)}, u32[]{:S(2)}, u32[]{:S(2)}) collective-permute-start(bf16[2,128,1024]{2,1,0:T(8,128)(2,1)S(1)} %get-tuple-element.171.da), channel_id=1, source_target_pairs={{0,1},{1,0},{2,3},{3,2},{4,5},{5,4},{6,7},{7,6},{8,9},{9,8},{10,11... | collective-permute-start | bytes 1572872 | tf_op jit(solution)/shard_map/ppermute | solution.py:30
  190.4 25.7 %all-to-all-start = ((bf16[16,16,1024]{2,1,0:T(8,128)(2,1)}), bf16[16,16,1024]{2,1,0:T(8,128)(2,1)S(1)}, u32[]{:S(2)}, u32[]{:S(2)}) async-start(bf16[16,16,1024]{2,1,0:T(8,128)(2,1)} %get-tuple-element.172), calls=%async_computation | async-start | bytes 1048576 | tf_op jit(solution)/shard_map/all_to_all | solution.py:329
  197.5 17.2 %collective-permute-start.32 = (bf16[2,32,1024]{2,1,0:T(8,128)(2,1)S(1)}, bf16[2,32,1024]{2,1,0:T(8,128)(2,1)S(1)}, u32[]{:S(2)}, u32[]{:S(2)}) collective-permute-start(bf16[2,32,1024]{2,1,0:T(8,128)(2,1)S(1)} %shard_map.79), channel_id=1, source_target_pairs={{64,65},{65,66},{66,67},{67,68},{68,69},{69,70},{70,71},{71,72},{7... | collective-permute-start | bytes 393224 | tf_op jit(solution)/shard_map/ppermute | solution.py:30
  209.3 13.7 %collective-permute-start.34 = (f32[16,1024]{1,0:T(8,128)S(1)}, f32[16,1024]{1,0:T(8,128)S(1)}, u32[]{:S(2)}, u32[]{:S(2)}) collective-permute-start(f32[16,1024]{1,0:T(8,128)S(1)} %shard_map.82), channel_id=1, source_target_pairs={{0,8},{1,9},{2,10},{3,11},{4,12},{5,13},{6,14},{7,15},{8,0},{9,1},... | collective-permute-start | bytes 196616 | tf_op jit(solution)/shard_map/ppermute | solution.py:30
  (16 other events, 32.5 us)

commit v4 on v3

--- a/solution.py
+++ b/solution.py
@@ -176,10 +176,18 @@
     micro, rows, width = z.shape
     z_t = z[...].reshape(micro * rows, width).T
     even = flags[EVEN] == 1
-    for q in range(width // 32):
-        a, b = z_t[32 * q : 32 * q + 16], z_t[32 * q + 16 : 32 * q + 32]
-        mine[16 * q : 16 * q + 16, :] = jnp.where(even, a, b)
-        other[16 * q : 16 * q + 16, :] = jnp.where(even, b, a)
+    upper = flags[LOWER] == 1
+    half = mine.shape[0] // 2
+    for y in range(4):
+        for x in range(4):
+            pair = []
+            for q in (8 * y + x, 8 * y + 4 + x):
+                a, b = z_t[32 * q : 32 * q + 16], z_t[32 * q + 16 : 32 * q + 32]
+                pair.append((jnp.where(even, a, b), jnp.where(even, b, a)))
+            place = 16 * (4 * y + x)
+            for out, low, high in zip((mine, other), *pair):
+                out[place : place + 16, :] = jnp.where(upper, low, high)
+                out[half + place : half + place + 16, :] = jnp.where(upper, high, low)
 
 
 def weight_kernel(flags, za, zb, da, db, far, near):
@@ -189,12 +197,9 @@
         zb[...], db[...].reshape(micro * rows, width), preferred_element_type=f32
     )
     total = total.astype(bf16)
-    upper = flags[LOWER] == 1
-    for y in range(4):
-        for x in range(4):
-            a, b = (total[16 * q : 16 * q + 16] for q in (8 * y + x, 8 * y + 4 + x))
-            far[4 * y + x] = jnp.where(upper, a, b)
-            near[4 * y + x] = jnp.where(upper, b, a)
+    half = total.shape[0] // 2
+    far[...] = total[:half].reshape(far.shape)
+    near[...] = total[half:].reshape(near.shape)
 
 
 def sum_kernel(flags, parts, out):
@@ -266,6 +271,8 @@
     ty = permute(ty, edges(1, top, 0))
     from_x = permute(from_x, swap(1))
     (w_t,) = call(turn_kernel, [((width, width), bf16)], flags, [w])
+    w_t, y_pack = lax.optimization_barrier((w_t, y_pack))
+    ry = permute(y_pack, edges(1, rest, 0))
     field = ((micro, rows, width), bf16)
     made = [((micro, span, width), f32), ((reach, span), bf16), field]
 
@@ -283,8 +290,7 @@
     received = [[upstream, from_x, ty]] * micro
     for layer in reversed(range(sections)):
         if layer == rest[-1]:
-            y_pack, grads, *prepared = lax.optimization_barrier((y_pack, grads, *prepared))
-            ry = permute(y_pack, edges(1, rest, 0))
+            grads, *prepared = lax.optimization_barrier((grads, *prepared))
             prepared = prepare(REST, (from_x, ry), prepared)
         if layer == rest[-1] - 1:
             half_shape = ((width // 2, micro * rows), bf16)

time: 225 us -> 224 us (level)
  blocking collectives: 25.2 us -> 20.3 us
  starting transfers between devices: 76.1 us -> 78.4 us
    all_to_all x1, blocking collectives: 25.2 us -> 20.3 us  [shards(): far = lax.all_to_all(far, 'space', 0, 0, axis_index_groups=groups)]
    ppermute x35, starting transfers between devices: 69 us -> 71.4 us  [permute(): return lax.ppermute(value, AXES, pairs)]
  transfers between devices with their start and end apart: 36 -> 36, of which waited for: 6 -> 6; matrix products, arithmetic and copies ran while one was open for 0% -> 0% of each run, Pallas kernels for 6% -> 7%
where the time goes in v4:
time: 224 us; the launch traced here: 223 us
  waiting for transfers between devices  97.1 us (43%)
  starting transfers between devices  78.4 us (35%)
  Pallas kernels  22.1 us (10%)
  blocking collectives  20.3 us (9%)
  local copies, waits for them, and re-layouts  3.91 us (2%)
    ppermute x35, waiting for transfers between devices, permute(): return lax.ppermute(value, AXES, pairs)  97.1 us
    ppermute x35, starting transfers between devices, permute(): return lax.ppermute(value, AXES, pairs)  71.4 us
    all_to_all x1, blocking collectives, shards(): far = lax.all_to_all(far, 'space', 0, 0, axis_index_groups=groups)  20.3 us
    pallas_call x25, Pallas kernels, call(): pl.pallas_call(kernel, out_shape=tuple((pltpu.VMEM(shape, dtype) for shap...  20.1 us
    all_to_all x1, starting transfers between devices, shards(): close = lax.all_to_all(close, 'space', 0, 0, axis_index_groups=groups)  7.06 us
  transfers between devices with their start and end apart: 36, of which 6 were waited for; matrix products, arithmetic and copies ran while one was open for 0% of the time, Pallas kernels for 7%

profile of v4, /device:TPU:47, one launch (start us, length us, event | category | flops | bytes accessed | tf_op | source)
XLA Modules:
  0.0 223.3 jit_solution(8106997412165951239)
XLA Ops:
  1.6 1.9 pack.1
  3.5 2.6 %collective-permute-start = (bf16[336,1024]{1,0:T(8,128)(2,1)S(1)}, bf16[336,1024]{1,0:T(8,128)(2,1)S(1)}, u32[]{:S(2)}, u32[]{:S(2)}) collective-permute-start(bf16[336,1024]{1,0:T(8,128)(2,1)S(1)} %get-tuple-element.91), channel_id=1, source_target_pairs={{0,1},{1,0},{2,3},{3,2},{4,5},{5,4},{6,7},{7,6},{8,9},{9,8},{10,11... | collective-permute-start | bytes 2064392 | tf_op jit(solution)/shard_map/ppermute | solution.py:30
  6.8 1.6 copy-done
  9.6 14.5 %collective-permute-start.4 = (bf16[208,1024]{1,0:T(8,128)(2,1)S(1)}, bf16[208,1024]{1,0:T(8,128)(2,1)S(1)}, u32[]{:S(2)}, u32[]{:S(2)}) collective-permute-start(bf16[208,1024]{1,0:T(8,128)(2,1)S(1)} %get-tuple-element.103), channel_id=1, source_target_pairs={{0,63},{1,2},{2,1},{3,4},{4,3},{5,6},{6,5},{7,8},{8,7},{9,10},{10,... | collective-permute-start | bytes 1277960 | tf_op jit(solution)/shard_map/ppermute | solution.py:30
  28.6 15.9 %collective-permute-done.4.from_y = bf16[208,1024]{1,0:T(8,128)(2,1)S(1)} collective-permute-done((bf16[208,1024]{1,0:T(8,128)(2,1)S(1)}, bf16[208,1024]{1,0:T(8,128)(2,1)S(1)}, u32[]{:S(2)}, u32[]{:S(2)}) %collective-permute-start.4) | collective-permute-done | bytes 426016 | tf_op jit(solution)/shard_map/ppermute | solution.py:30
  44.5 3.1 %shard_map.63 = (f32[2,256,1024]{2,1,0:T(8,128)S(1)}, bf16[320,256]{1,0:T(8,128)(2,1)S(1)}, bf16[2,128,1024]{2,1,0:T(8,128)(2,1)S(1)}) custom-call(s32[13]{0:T(128)S(1)} %concatenate.3.flags, bf16[2,128,1024]{2,1,0:T(8,128)(2,1)S(1)} %bitcast.15, ...), custom_call_target="tpu_custom_call", output_to_operand_aliasing={{0}: (6, {}), {1}: (7, {}), {2}: (8, {})} | custom-call | tf_op jit(solution)/shard_map/pallas_call | solution.py:34
  49.5 1.9 collective-permute-start.11
  66.5 1.3 collective-permute-start.26
  68.4 1.3 collective-permute-start.24
  69.7 1.3 collective-permute-start.27
  71.0 1.3 collective-permute-start.25
  72.3 71.2 %collective-permute-done.27.refs_1_ = bf16[64,1024]{1,0:T(8,128)(2,1)S(1)} collective-permute-done((bf16[64,1024]{1,0:T(8,128)(2,1)S(1)}, bf16[64,1024]{1,0:T(8,128)(2,1)S(1)}, u32[]{:S(2)}, u32[]{:S(2)}) %collective-permute-start.27) | collective-permute-done | bytes 131104 | tf_op jit(solution)/shard_map/ppermute | solution.py:30
  144.6 1.3 collective-permute-start.30
  147.1 1.3 collective-permute-start.28
  148.4 1.3 collective-permute-start.31
  149.7 1.3 collective-permute-start.29
  154.2 11.3 %collective-permute-start.33 = (bf16[2,128,1024]{2,1,0:T(8,128)(2,1)S(1)}, bf16[2,128,1024]{2,1,0:T(8,128)(2,1)S(1)}, u32[]{:S(2)}, u32[]{:S(2)}) collective-permute-start(bf16[2,128,1024]{2,1,0:T(8,128)(2,1)S(1)} %get-tuple-element.173.da), channel_id=1, source_target_pairs={{0,1},{1,0},{2,3},{3,2},{4,5},{5,4},{6,7},{7,6},{8,9},{9,8},{10,11... | collective-permute-start | bytes 1572872 | tf_op jit(solution)/shard_map/ppermute | solution.py:30
  165.5 1.5 collective-permute-done.33.db
  167.0 2.1 shard_map.81
  169.1 20.3 %all_to_all.10.parts = bf16[16,16,1024]{2,1,0:T(8,128)(2,1)S(1)} all-to-all(bf16[16,16,1024]{2,1,0:T(8,128)(2,1)S(1)} %get-tuple-element.175), channel_id=1, replica_groups={{0,2,4,6,16,18,20,22,32,34,36,38,48,50,52,54},{1,3,5,7,17,19,21,23,33,3..., dimensions={0} | all-to-all | bytes 1048576 | tf_op jit(solution)/shard_map/all_to_all | solution.py:334
  189.4 7.1 %all-to-all-start = ((bf16[16,16,1024]{2,1,0:T(8,128)(2,1)}), bf16[16,16,1024]{2,1,0:T(8,128)(2,1)S(1)}, u32[]{:S(2)}, u32[]{:S(2)}) async-start(bf16[16,16,1024]{2,1,0:T(8,128)(2,1)} %get-tuple-element.174), calls=%async_computation | async-start | bytes 1048576 | tf_op jit(solution)/shard_map/all_to_all | solution.py:335
  196.5 11.2 %collective-permute-start.32 = (bf16[2,32,1024]{2,1,0:T(8,128)(2,1)S(1)}, bf16[2,32,1024]{2,1,0:T(8,128)(2,1)S(1)}, u32[]{:S(2)}, u32[]{:S(2)}) collective-permute-start(bf16[2,32,1024]{2,1,0:T(8,128)(2,1)S(1)} %shard_map.79), channel_id=1, source_target_pairs={{64,65},{65,66},{66,67},{67,68},{68,69},{69,70},{70,71},{71,72},{7... | collective-permute-start | bytes 393224 | tf_op jit(solution)/shard_map/ppermute | solution.py:30
  208.3 5.4 %collective-permute-start.34 = (f32[16,1024]{1,0:T(8,128)S(1)}, f32[16,1024]{1,0:T(8,128)S(1)}, u32[]{:S(2)}, u32[]{:S(2)}) collective-permute-start(f32[16,1024]{1,0:T(8,128)S(1)} %shard_map.82), channel_id=1, source_target_pairs={{0,8},{1,9},{2,10},{3,11},{4,12},{5,13},{6,14},{7,15},{8,0},{9,1},... | collective-permute-start | bytes 196616 | tf_op jit(solution)/shard_map/ppermute | solution.py:30
  215.1 6.9 %collective-permute-done.34.other = f32[16,1024]{1,0:T(8,128)S(1)} collective-permute-done((f32[16,1024]{1,0:T(8,128)S(1)}, f32[16,1024]{1,0:T(8,128)S(1)}, u32[]{:S(2)}, u32[]{:S(2)}) %collective-permute-start.34) | collective-permute-done | bytes 65568 | tf_op jit(solution)/shard_map/ppermute | solution.py:30
  (88 shorter events, 33.1 us)
Async XLA Ops:
  3.5 20.6 %collective-permute-start = (bf16[336,1024]{1,0:T(8,128)(2,1)S(1)}, bf16[336,1024]{1,0:T(8,128)(2,1)S(1)}, u32[]{:S(2)}, u32[]{:S(2)}) collective-permute-start(bf16[336,1024]{1,0:T(8,128)(2,1)S(1)} %get-tuple-element.91), channel_id=1, source_target_pairs={{0,1},{1,0},{2,3},{3,2},{4,5},{5,4},{6,7},{7,6},{8,9},{9,8},{10,11... | collective-permute-start | bytes 2064392 | tf_op jit(solution)/shard_map/ppermute | solution.py:30
  6.1 18.0 %collective-permute-start.1 = (bf16[336,1024]{1,0:T(8,128)(2,1)S(1)}, bf16[336,1024]{1,0:T(8,128)(2,1)S(1)}, u32[]{:S(2)}, u32[]{:S(2)}) collective-permute-start(bf16[336,1024]{1,0:T(8,128)(2,1)S(1)} %get-tuple-element.92), channel_id=1, source_target_pairs={{448,511},{449,450},{450,449},{451,452},{452,451},{453,454},{454,4... | collective-permute-start | bytes 2064392 | tf_op jit(solution)/shard_map/ppermute | solution.py:30
  9.6 34.8 %collective-permute-start.4 = (bf16[208,1024]{1,0:T(8,128)(2,1)S(1)}, bf16[208,1024]{1,0:T(8,128)(2,1)S(1)}, u32[]{:S(2)}, u32[]{:S(2)}) collective-permute-start(bf16[208,1024]{1,0:T(8,128)(2,1)S(1)} %get-tuple-element.103), channel_id=1, source_target_pairs={{0,63},{1,2},{2,1},{3,4},{4,3},{5,6},{6,5},{7,8},{8,7},{9,10},{10,... | collective-permute-start | bytes 1277960 | tf_op jit(solution)/shard_map/ppermute | solution.py:30
  25.3 22.3 %collective-permute-start.5 = (bf16[128,1024]{1,0:T(8,128)(2,1)S(1)}, bf16[128,1024]{1,0:T(8,128)(2,1)S(1)}, u32[]{:S(2)}, u32[]{:S(2)}) collective-permute-start(bf16[128,1024]{1,0:T(8,128)(2,1)S(1)} %get-tuple-element.111), channel_id=1, source_target_pairs={{448,384},{449,385},{450,386},{451,387},{452,388},{453,389},{454,3... | collective-permute-start | bytes 786440 | tf_op jit(solution)/shard_map/ppermute | solution.py:30
  26.5 21.6 %collective-permute-start.2 = (bf16[128,1024]{1,0:T(8,128)(2,1)S(1)}, bf16[128,1024]{1,0:T(8,128)(2,1)S(1)}, u32[]{:S(2)}, u32[]{:S(2)}) collective-permute-start(bf16[128,1024]{1,0:T(8,128)(2,1)S(1)} %get-tuple-element.101), channel_id=1, source_target_pairs={{448,384},{449,385},{450,386},{451,387},{452,388},{453,389},{454,3... | collective-permute-start | bytes 786440 | tf_op jit(solution)/shard_map/ppermute | solution.py:30
  27.2 20.3 %collective-permute-start.6 = (bf16[64,1024]{1,0:T(8,128)(2,1)S(1)}, bf16[64,1024]{1,0:T(8,128)(2,1)S(1)}, u32[]{:S(2)}, u32[]{:S(2)}) collective-permute-start(bf16[64,1024]{1,0:T(8,128)(2,1)S(1)} %get-tuple-element.112), channel_id=1, source_target_pairs={{448,385},{449,386},{450,387},{451,388},{452,389},{453,390},{454,3... | collective-permute-start | bytes 393224 | tf_op jit(solution)/shard_map/ppermute | solution.py:30
  27.9 20.2 %collective-permute-start.3 = (bf16[64,1024]{1,0:T(8,128)(2,1)S(1)}, bf16[64,1024]{1,0:T(8,128)(2,1)S(1)}, u32[]{:S(2)}, u32[]{:S(2)}) collective-permute-start(bf16[64,1024]{1,0:T(8,128)(2,1)S(1)} %get-tuple-element.102), channel_id=1, source_target_pairs={{448,385},{449,386},{450,387},{451,388},{452,389},{453,390},{454,3... | collective-permute-start | bytes 393224 | tf_op jit(solution)/shard_map/ppermute | solution.py:30
  49.5 4.7 %collective-permute-start.11 = (bf16[512,256]{1,0:T(8,128)(2,1)S(1)}, bf16[512,256]{1,0:T(8,128)(2,1)S(1)}, u32[]{:S(2)}, u32[]{:S(2)}) collective-permute-start(bf16[512,256]{1,0:T(8,128)(2,1)S(1)} %get-tuple-element.125), channel_id=1, source_target_pairs={{0,1},{1,0},{2,3},{3,2},{4,5},{5,4},{6,7},{7,6},{8,9},{9,8},{10,11... | collective-permute-start | bytes 786440 | tf_op jit(solution)/shard_map/ppermute | solution.py:30
  52.1 3.3 %collective-permute-start.7 = (bf16[128,1024]{1,0:T(8,128)(2,1)S(1)}, bf16[128,1024]{1,0:T(8,128)(2,1)S(1)}, u32[]{:S(2)}, u32[]{:S(2)}) collective-permute-start(bf16[128,1024]{1,0:T(8,128)(2,1)S(1)} %get-tuple-element.117), channel_id=1, source_target_pairs={{384,320},{385,321},{386,322},{387,323},{388,324},{389,325},{390,3... | collective-permute-start | bytes 786440 | tf_op jit(solution)/shard_map/ppermute | solution.py:30
  54.7 3.3 %collective-permute-start.14 = (bf16[128,1024]{1,0:T(8,128)(2,1)S(1)}, bf16[128,1024]{1,0:T(8,128)(2,1)S(1)}, u32[]{:S(2)}, u32[]{:S(2)}) collective-permute-start(bf16[128,1024]{1,0:T(8,128)(2,1)S(1)} %get-tuple-element.132), channel_id=1, source_target_pairs={{320,256},{321,257},{322,258},{323,259},{324,260},{325,261},{326,2... | collective-permute-start | bytes 786440 | tf_op jit(solution)/shard_map/ppermute | solution.py:30
  62.5 3.5 %collective-permute-start.22 = (bf16[128,1024]{1,0:T(8,128)(2,1)S(1)}, bf16[128,1024]{1,0:T(8,128)(2,1)S(1)}, u32[]{:S(2)}, u32[]{:S(2)}) collective-permute-start(bf16[128,1024]{1,0:T(8,128)(2,1)S(1)} %get-tuple-element.148), channel_id=1, source_target_pairs={{192,128},{193,129},{194,130},{195,131},{196,132},{197,133},{198,1... | collective-permute-start | bytes 786440 | tf_op jit(solution)/shard_map/ppermute | solution.py:30
  63.9 3.9 %collective-permute-start.20 = (bf16[128,1024]{1,0:T(8,128)(2,1)S(1)}, bf16[128,1024]{1,0:T(8,128)(2,1)S(1)}, u32[]{:S(2)}, u32[]{:S(2)}) collective-permute-start(bf16[128,1024]{1,0:T(8,128)(2,1)S(1)} %get-tuple-element.146), channel_id=1, source_target_pairs={{192,128},{193,129},{194,130},{195,131},{196,132},{197,133},{198,1... | collective-permute-start | bytes 786440 | tf_op jit(solution)/shard_map/ppermute | solution.py:30
  66.5 76.9 %collective-permute-start.26 = (bf16[128,1024]{1,0:T(8,128)(2,1)S(1)}, bf16[128,1024]{1,0:T(8,128)(2,1)S(1)}, u32[]{:S(2)}, u32[]{:S(2)}) collective-permute-start(bf16[128,1024]{1,0:T(8,128)(2,1)S(1)} %get-tuple-element.156), channel_id=1, source_target_pairs={{128,64},{129,65},{130,66},{131,67},{132,68},{133,69},{134,70},{13... | collective-permute-start | bytes 786440 | tf_op jit(solution)/shard_map/ppermute | solution.py:30
  68.4 77.5 %collective-permute-start.24 = (bf16[128,1024]{1,0:T(8,128)(2,1)S(1)}, bf16[128,1024]{1,0:T(8,128)(2,1)S(1)}, u32[]{:S(2)}, u32[]{:S(2)}) collective-permute-start(bf16[128,1024]{1,0:T(8,128)(2,1)S(1)} %get-tuple-element.154), channel_id=1, source_target_pairs={{128,64},{129,65},{130,66},{131,67},{132,68},{133,69},{134,70},{13... | collective-permute-start | bytes 786440 | tf_op jit(solution)/shard_map/ppermute | solution.py:30
  69.7 73.8 %collective-permute-start.27 = (bf16[64,1024]{1,0:T(8,128)(2,1)S(1)}, bf16[64,1024]{1,0:T(8,128)(2,1)S(1)}, u32[]{:S(2)}, u32[]{:S(2)}) collective-permute-start(bf16[64,1024]{1,0:T(8,128)(2,1)S(1)} %get-tuple-element.157), channel_id=1, source_target_pairs={{128,127},{129,64},{130,65},{131,66},{132,67},{133,68},{134,69},{1... | collective-permute-start | bytes 393224 | tf_op jit(solution)/shard_map/ppermute | solution.py:30
  71.0 74.9 %collective-permute-start.25 = (bf16[64,1024]{1,0:T(8,128)(2,1)S(1)}, bf16[64,1024]{1,0:T(8,128)(2,1)S(1)}, u32[]{:S(2)}, u32[]{:S(2)}) collective-permute-start(bf16[64,1024]{1,0:T(8,128)(2,1)S(1)} %get-tuple-element.155), channel_id=1, source_target_pairs={{128,127},{129,64},{130,65},{131,66},{132,67},{133,68},{134,69},{1... | collective-permute-start | bytes 393224 | tf_op jit(solution)/shard_map/ppermute | solution.py:30
  144.6 7.7 %collective-permute-start.30 = (bf16[128,1024]{1,0:T(8,128)(2,1)S(1)}, bf16[128,1024]{1,0:T(8,128)(2,1)S(1)}, u32[]{:S(2)}, u32[]{:S(2)}) collective-permute-start(bf16[128,1024]{1,0:T(8,128)(2,1)S(1)} %get-tuple-element.164), channel_id=1, source_target_pairs={{64,0},{65,1},{66,2},{67,3},{68,4},{69,5},{70,6},{71,7},{72,8},{73... | collective-permute-start | bytes 786440 | tf_op jit(solution)/shard_map/ppermute | solution.py:30
  147.1 6.6 %collective-permute-start.28 = (bf16[128,1024]{1,0:T(8,128)(2,1)S(1)}, bf16[128,1024]{1,0:T(8,128)(2,1)S(1)}, u32[]{:S(2)}, u32[]{:S(2)}) collective-permute-start(bf16[128,1024]{1,0:T(8,128)(2,1)S(1)} %get-tuple-element.162), channel_id=1, source_target_pairs={{64,0},{65,1},{66,2},{67,3},{68,4},{69,5},{70,6},{71,7},{72,8},{73... | collective-permute-start | bytes 786440 | tf_op jit(solution)/shard_map/ppermute | solution.py:30
  148.4 3.9 %collective-permute-start.31 = (bf16[64,1024]{1,0:T(8,128)(2,1)S(1)}, bf16[64,1024]{1,0:T(8,128)(2,1)S(1)}, u32[]{:S(2)}, u32[]{:S(2)}) collective-permute-start(bf16[64,1024]{1,0:T(8,128)(2,1)S(1)} %get-tuple-element.165), channel_id=1, source_target_pairs={{64,1},{65,2},{66,3},{67,4},{68,5},{69,6},{70,7},{71,8},{72,9},{73... | collective-permute-start | bytes 393224 | tf_op jit(solution)/shard_map/ppermute | solution.py:30
  149.7 4.0 %collective-permute-start.29 = (bf16[64,1024]{1,0:T(8,128)(2,1)S(1)}, bf16[64,1024]{1,0:T(8,128)(2,1)S(1)}, u32[]{:S(2)}, u32[]{:S(2)}) collective-permute-start(bf16[64,1024]{1,0:T(8,128)(2,1)S(1)} %get-tuple-element.163), channel_id=1, source_target_pairs={{64,1},{65,2},{66,3},{67,4},{68,5},{69,6},{70,7},{71,8},{72,9},{73... | collective-permute-start | bytes 393224 | tf_op jit(solution)/shard_map/ppermute | solution.py:30
  154.2 12.8 %collective-permute-start.33 = (bf16[2,128,1024]{2,1,0:T(8,128)(2,1)S(1)}, bf16[2,128,1024]{2,1,0:T(8,128)(2,1)S(1)}, u32[]{:S(2)}, u32[]{:S(2)}) collective-permute-start(bf16[2,128,1024]{2,1,0:T(8,128)(2,1)S(1)} %get-tuple-element.173.da), channel_id=1, source_target_pairs={{0,1},{1,0},{2,3},{3,2},{4,5},{5,4},{6,7},{7,6},{8,9},{9,8},{10,11... | collective-permute-start | bytes 1572872 | tf_op jit(solution)/shard_map/ppermute | solution.py:30
  189.4 25.7 %all-to-all-start = ((bf16[16,16,1024]{2,1,0:T(8,128)(2,1)}), bf16[16,16,1024]{2,1,0:T(8,128)(2,1)S(1)}, u32[]{:S(2)}, u32[]{:S(2)}) async-start(bf16[16,16,1024]{2,1,0:T(8,128)(2,1)} %get-tuple-element.174), calls=%async_computation | async-start | bytes 1048576 | tf_op jit(solution)/shard_map/all_to_all | solution.py:335
  196.5 17.2 %collective-permute-start.32 = (bf16[2,32,1024]{2,1,0:T(8,128)(2,1)S(1)}, bf16[2,32,1024]{2,1,0:T(8,128)(2,1)S(1)}, u32[]{:S(2)}, u32[]{:S(2)}) collective-permute-start(bf16[2,32,1024]{2,1,0:T(8,128)(2,1)S(1)} %shard_map.79), channel_id=1, source_target_pairs={{64,65},{65,66},{66,67},{67,68},{68,69},{69,70},{70,71},{71,72},{7... | collective-permute-start | bytes 393224 | tf_op jit(solution)/shard_map/ppermute | solution.py:30
  208.3 13.7 %collective-permute-start.34 = (f32[16,1024]{1,0:T(8,128)S(1)}, f32[16,1024]{1,0:T(8,128)S(1)}, u32[]{:S(2)}, u32[]{:S(2)}) collective-permute-start(f32[16,1024]{1,0:T(8,128)S(1)} %shard_map.82), channel_id=1, source_target_pairs={{0,8},{1,9},{2,10},{3,11},{4,12},{5,13},{6,14},{7,15},{8,0},{9,1},... | collective-permute-start | bytes 196616 | tf_op jit(solution)/shard_map/ppermute | solution.py:30
  (16 other events, 74.7 us)

commit v5 on v4

--- a/solution.py
+++ b/solution.py
@@ -128,7 +128,10 @@
 def layer_kernel(layer, m, sources, olds, flags, *refs):
     g_in = refs[:sources]
     factor, mix, w_t = refs[sources : sources + 3]
-    grads, kept, *sends = refs[sources + 3 + olds :]
+    grads, *sends = refs[sources + 3 + olds :]
+    kept = None
+    if not (layer == 0 and m == 1):
+        kept, *sends = sends
     micro, rows, width = grads.shape
     span = rows + EDGE
     odd = layer % 2 == 1
@@ -144,7 +147,8 @@
         g_field = jnp.concatenate([own, edge] if odd else [edge, own], axis=0)
         first = EDGE if odd else HALO
         du = (g_field.astype(f32) * factor[m, first : first + span, :]).astype(bf16)
-        kept[m] = du[EDGE - first : EDGE - first + rows]
+        if kept is not None:
+            kept[m] = du[EDGE - first : EDGE - first + rows]
         blank = [jnp.zeros((n, width), bf16) for n in (first, mix.shape[1] - span - first)]
         parts = [p for p in (blank[0], du, blank[1]) if p.shape[0]]
         above = WIDE + (HALO if odd else 0)
@@ -158,6 +162,16 @@
         if sends:
             sends[0][...] = total
             sends[1][...] = total[rows - EDGE :] if odd else total[:EDGE]
+
+
+def last_du_kernel(m, flags, main, edge, factor, old, kept):
+    rows = main.shape[0]
+
+    @pl.when(flags[0] == 1)
+    def _():
+        g_field = jnp.concatenate([edge[EDGE - HALO :, :], main[: rows - HALO, :]], axis=0)
+        du = g_field.astype(f32) * factor[m, EDGE : EDGE + rows, :]
+        kept[m] = du.astype(bf16)
 
 
 def rim_kernel(flags, grads, out):
@@ -190,10 +204,14 @@
                 out[half + place : half + place + 16, :] = jnp.where(upper, high, low)
 
 
-def weight_kernel(flags, za, zb, da, db, far, near):
+def own_weight_kernel(flags, za, da, out):
     micro, rows, width = da.shape
-    total = jnp.dot(za[...], da[...].reshape(micro * rows, width), preferred_element_type=f32)
-    total = total + jnp.dot(
+    out[...] = jnp.dot(za[...], da[...].reshape(micro * rows, width), preferred_element_type=f32)
+
+
+def weight_kernel(flags, own, zb, db, far, near):
+    micro, rows, width = db.shape
+    total = own[...] + jnp.dot(
         zb[...], db[...].reshape(micro * rows, width), preferred_element_type=f32
     )
     total = total.astype(bf16)
@@ -301,6 +319,24 @@
         factor, mix, _ = prepared
         arriving = []
         for m in range(micro):
+            last = layer == 0 and m == micro - 1
+            if last:
+                (kept,) = call(
+                    functools.partial(last_du_kernel, m),
+                    [field],
+                    flags,
+                    [*received[m], factor, kept],
+                    {4: 0},
+                )
+                du_other = permute(kept, swap(1))
+                (grads,) = call(
+                    functools.partial(layer_kernel, layer, m, len(received[m]), 1),
+                    [field],
+                    flags,
+                    [*received[m], factor, mix, w_t, grads],
+                    {4 + len(received[m]): 0},
+                )
+                continue
             old = [] if grads is None else [grads, kept]
             sent = [((r, width), bf16) for r in (rows, EDGE)] if layer else []
             first = 4 + len(received[m])
@@ -321,11 +357,9 @@
             (rim,) = call(rim_kernel, [((micro, HALO, width), bf16)], flags, [grads])
             rim = permute(rim, toward(range(1, sections, 2), 0, 1))
 
-    du_other = permute(kept, swap(1))
     slab = (width // count, width)
-    far, close = call(
-        weight_kernel, [((16, *slab), bf16)] * 2, flags, [mine, other, kept, du_other]
-    )
+    (own,) = call(own_weight_kernel, [((width // 2, width), f32)], flags, [mine, kept])
+    far, close = call(weight_kernel, [((16, *slab), bf16)] * 2, flags, [own, other, du_other])
     groups = [
         [16 * y + 8 * z + 2 * x + c for y in range(4) for x in range(4)]
         for z in range(2)

time: 224 us -> 225 us (level)
  waiting for transfers between devices: 97.1 us -> 93.3 us
  local copies, waits for them, and re-layouts: 3.91 us -> 7.49 us
    ppermute x35, waiting for transfers between devices: 97.1 us -> 93.3 us  [permute(): return lax.ppermute(value, AXES, pairs)]
    unnamed x11 -> x25, local copies, waits for them, and re-layouts: 3.82 us -> 7.41 us
    pallas_call x25 -> x27, Pallas kernels: 20.1 us -> 21.2 us  [call(): pl.pallas_call(kernel, out_shape=tuple((pltpu.VMEM(shape, dtype) for shap...]
  transfers between devices with their start and end apart: 36 -> 36, of which waited for: 6 -> 7; matrix products, arithmetic and copies ran while one was open for 0% -> 0% of each run, Pallas kernels for 7% -> 8%
where the time goes in v5:
time: 225 us; the launch traced here: 224 us
  waiting for transfers between devices  93.3 us (41%)
  starting transfers between devices  77 us (34%)
  Pallas kernels  23.1 us (10%)
  blocking collectives  21.8 us (10%)
  local copies, waits for them, and re-layouts  7.49 us (3%)
    ppermute x35, waiting for transfers between devices, permute(): return lax.ppermute(value, AXES, pairs)  93.3 us
    ppermute x35, starting transfers between devices, permute(): return lax.ppermute(value, AXES, pairs)  69.9 us
    all_to_all x1, blocking collectives, shards(): far = lax.all_to_all(far, 'space', 0, 0, axis_index_groups=groups)  21.8 us
    pallas_call x27, Pallas kernels, call(): pl.pallas_call(kernel, out_shape=tuple((pltpu.VMEM(shape, dtype) for shap...  21.2 us
    unnamed x25, local copies, waits for them, and re-layouts  7.41 us
    all_to_all x1, starting transfers between devices, shards(): close = lax.all_to_all(close, 'space', 0, 0, axis_index_groups=groups)  7.06 us
  transfers between devices with their start and end apart: 36, of which 7 were waited for; matrix products, arithmetic and copies ran while one was open for 0% of the time, Pallas kernels for 8%

profile of v5, /device:TPU:47, one launch (start us, length us, event | category | flops | bytes accessed | tf_op | source)
XLA Modules:
  0.0 224.2 jit_solution(1094607493649421693)
XLA Ops:
  1.6 1.9 pack.1
  3.5 2.6 %collective-permute-start = (bf16[336,1024]{1,0:T(8,128)(2,1)S(1)}, bf16[336,1024]{1,0:T(8,128)(2,1)S(1)}, u32[]{:S(2)}, u32[]{:S(2)}) collective-permute-start(bf16[336,1024]{1,0:T(8,128)(2,1)S(1)} %get-tuple-element.89), channel_id=1, source_target_pairs={{0,1},{1,0},{2,3},{3,2},{4,5},{5,4},{6,7},{7,6},{8,9},{9,8},{10,11... | collective-permute-start | bytes 2064392 | tf_op jit(solution)/shard_map/ppermute | solution.py:30
  6.8 1.6 copy-done.2
  9.6 14.5 %collective-permute-start.4 = (bf16[208,1024]{1,0:T(8,128)(2,1)S(1)}, bf16[208,1024]{1,0:T(8,128)(2,1)S(1)}, u32[]{:S(2)}, u32[]{:S(2)}) collective-permute-start(bf16[208,1024]{1,0:T(8,128)(2,1)S(1)} %get-tuple-element.101), channel_id=1, source_target_pairs={{0,63},{1,2},{2,1},{3,4},{4,3},{5,6},{6,5},{7,8},{8,7},{9,10},{10,... | collective-permute-start | bytes 1277960 | tf_op jit(solution)/shard_map/ppermute | solution.py:30
  28.6 15.9 %collective-permute-done.4.from_y = bf16[208,1024]{1,0:T(8,128)(2,1)S(1)} collective-permute-done((bf16[208,1024]{1,0:T(8,128)(2,1)S(1)}, bf16[208,1024]{1,0:T(8,128)(2,1)S(1)}, u32[]{:S(2)}, u32[]{:S(2)}) %collective-permute-start.4) | collective-permute-done | bytes 426016 | tf_op jit(solution)/shard_map/ppermute | solution.py:30
  44.5 3.1 %shard_map.63 = (f32[2,256,1024]{2,1,0:T(8,128)S(1)}, bf16[320,256]{1,0:T(8,128)(2,1)S(1)}, bf16[2,128,1024]{2,1,0:T(8,128)(2,1)S(1)}) custom-call(s32[13]{0:T(128)S(1)} %concatenate.3.flags, bf16[2,128,1024]{2,1,0:T(8,128)(2,1)S(1)} %bitcast.15, ...), custom_call_target="tpu_custom_call", output_to_operand_aliasing={{0}: (6, {}), {1}: (7, {}), {2}: (8, {})} | custom-call | tf_op jit(solution)/shard_map/pallas_call | solution.py:34
  49.5 1.9 collective-permute-start.11
  66.6 1.3 collective-permute-start.26
  68.4 1.3 collective-permute-start.24
  69.7 1.3 collective-permute-start.27
  72.3 69.7 %collective-permute-done.27.refs_1_ = bf16[64,1024]{1,0:T(8,128)(2,1)S(1)} collective-permute-done((bf16[64,1024]{1,0:T(8,128)(2,1)S(1)}, bf16[64,1024]{1,0:T(8,128)(2,1)S(1)}, u32[]{:S(2)}, u32[]{:S(2)}) %collective-permute-start.27) | collective-permute-done | bytes 131104 | tf_op jit(solution)/shard_map/ppermute | solution.py:30
  143.2 1.3 collective-permute-start.30
  144.5 1.3 collective-permute-done.24.refs_0_
  147.0 1.3 collective-permute-start.28
  148.3 1.3 collective-permute-start.31
  149.6 1.3 collective-permute-start.29
  152.7 1.5 collective-permute-done.29.refs_1_.edge
  154.8 9.8 %collective-permute-start.33 = (bf16[2,128,1024]{2,1,0:T(8,128)(2,1)S(1)}, bf16[2,128,1024]{2,1,0:T(8,128)(2,1)S(1)}, u32[]{:S(2)}, u32[]{:S(2)}) collective-permute-start(bf16[2,128,1024]{2,1,0:T(8,128)(2,1)S(1)} %shard_map.81.da), channel_id=1, source_target_pairs={{0,1},{1,0},{2,3},{3,2},{4,5},{5,4},{6,7},{7,6},{8,9},{9,8},{10,11... | collective-permute-start | bytes 1572872 | tf_op jit(solution)/shard_map/ppermute | solution.py:30
  167.2 21.8 %all_to_all.10.parts = bf16[16,16,1024]{2,1,0:T(8,128)(2,1)} all-to-all(bf16[16,16,1024]{2,1,0:T(8,128)(2,1)S(1)} %get-tuple-element.171), channel_id=1, replica_groups={{0,2,4,6,16,18,20,22,32,34,36,38,48,50,52,54},{1,3,5,7,17,19,21,23,33,3..., dimensions={0} | all-to-all | bytes 1048576 | tf_op jit(solution)/shard_map/all_to_all | solution.py:368
  189.0 7.1 %all-to-all-start = ((bf16[16,16,1024]{2,1,0:T(8,128)(2,1)}), bf16[16,16,1024]{2,1,0:T(8,128)(2,1)S(1)}, u32[]{:S(2)}, u32[]{:S(2)}) async-start(bf16[16,16,1024]{2,1,0:T(8,128)(2,1)} %copy-done.9), calls=%async_computation | async-start | bytes 1048576 | tf_op jit(solution)/shard_map/all_to_all | solution.py:369
  196.1 10.7 %collective-permute-start.32 = (bf16[2,32,1024]{2,1,0:T(8,128)(2,1)}, bf16[2,32,1024]{2,1,0:T(8,128)(2,1)S(1)}, u32[]{:S(2)}, u32[]{:S(2)}) collective-permute-start(bf16[2,32,1024]{2,1,0:T(8,128)(2,1)} %copy-done.10), channel_id=1, source_target_pairs={{64,65},{65,66},{66,67},{67,68},{68,69},{69,70},{70,71},{71,72},{7... | collective-permute-start | bytes 393224 | tf_op jit(solution)/shard_map/ppermute | solution.py:30
  209.1 5.9 %collective-permute-start.34 = (f32[16,1024]{1,0:T(8,128)}, f32[16,1024]{1,0:T(8,128)S(1)}, u32[]{:S(2)}, u32[]{:S(2)}) collective-permute-start(f32[16,1024]{1,0:T(8,128)} %shard_map.84), channel_id=1, source_target_pairs={{0,8},{1,9},{2,10},{3,11},{4,12},{5,13},{6,14},{7,15},{8,0},{9,1},... | collective-permute-start | bytes 196616 | tf_op jit(solution)/shard_map/ppermute | solution.py:30
  215.0 1.6 copy-done.1
  219.5 3.5 %collective-permute-done.34.other = f32[16,1024]{1,0:T(8,128)S(1)} collective-permute-done((f32[16,1024]{1,0:T(8,128)}, f32[16,1024]{1,0:T(8,128)S(1)}, u32[]{:S(2)}, u32[]{:S(2)}) %collective-permute-start.34) | collective-permute-done | bytes 65568 | tf_op jit(solution)/shard_map/ppermute | solution.py:30
  (104 shorter events, 39.2 us)
Async XLA Ops:
  3.5 20.6 %collective-permute-start = (bf16[336,1024]{1,0:T(8,128)(2,1)S(1)}, bf16[336,1024]{1,0:T(8,128)(2,1)S(1)}, u32[]{:S(2)}, u32[]{:S(2)}) collective-permute-start(bf16[336,1024]{1,0:T(8,128)(2,1)S(1)} %get-tuple-element.89), channel_id=1, source_target_pairs={{0,1},{1,0},{2,3},{3,2},{4,5},{5,4},{6,7},{7,6},{8,9},{9,8},{10,11... | collective-permute-start | bytes 2064392 | tf_op jit(solution)/shard_map/ppermute | solution.py:30
  6.1 18.0 %collective-permute-start.1 = (bf16[336,1024]{1,0:T(8,128)(2,1)S(1)}, bf16[336,1024]{1,0:T(8,128)(2,1)S(1)}, u32[]{:S(2)}, u32[]{:S(2)}) collective-permute-start(bf16[336,1024]{1,0:T(8,128)(2,1)S(1)} %get-tuple-element.90), channel_id=1, source_target_pairs={{448,511},{449,450},{450,449},{451,452},{452,451},{453,454},{454,4... | collective-permute-start | bytes 2064392 | tf_op jit(solution)/shard_map/ppermute | solution.py:30
  9.6 34.9 %collective-permute-start.4 = (bf16[208,1024]{1,0:T(8,128)(2,1)S(1)}, bf16[208,1024]{1,0:T(8,128)(2,1)S(1)}, u32[]{:S(2)}, u32[]{:S(2)}) collective-permute-start(bf16[208,1024]{1,0:T(8,128)(2,1)S(1)} %get-tuple-element.101), channel_id=1, source_target_pairs={{0,63},{1,2},{2,1},{3,4},{4,3},{5,6},{6,5},{7,8},{8,7},{9,10},{10,... | collective-permute-start | bytes 1277960 | tf_op jit(solution)/shard_map/ppermute | solution.py:30
  25.3 22.3 %collective-permute-start.5 = (bf16[128,1024]{1,0:T(8,128)(2,1)S(1)}, bf16[128,1024]{1,0:T(8,128)(2,1)S(1)}, u32[]{:S(2)}, u32[]{:S(2)}) collective-permute-start(bf16[128,1024]{1,0:T(8,128)(2,1)S(1)} %get-tuple-element.109), channel_id=1, source_target_pairs={{448,384},{449,385},{450,386},{451,387},{452,388},{453,389},{454,3... | collective-permute-start | bytes 786440 | tf_op jit(solution)/shard_map/ppermute | solution.py:30
  26.5 21.6 %collective-permute-start.2 = (bf16[128,1024]{1,0:T(8,128)(2,1)S(1)}, bf16[128,1024]{1,0:T(8,128)(2,1)S(1)}, u32[]{:S(2)}, u32[]{:S(2)}) collective-permute-start(bf16[128,1024]{1,0:T(8,128)(2,1)S(1)} %get-tuple-element.99), channel_id=1, source_target_pairs={{448,384},{449,385},{450,386},{451,387},{452,388},{453,389},{454,3... | collective-permute-start | bytes 786440 | tf_op jit(solution)/shard_map/ppermute | solution.py:30
  27.2 20.3 %collective-permute-start.6 = (bf16[64,1024]{1,0:T(8,128)(2,1)S(1)}, bf16[64,1024]{1,0:T(8,128)(2,1)S(1)}, u32[]{:S(2)}, u32[]{:S(2)}) collective-permute-start(bf16[64,1024]{1,0:T(8,128)(2,1)S(1)} %get-tuple-element.110), channel_id=1, source_target_pairs={{448,385},{449,386},{450,387},{451,388},{452,389},{453,390},{454,3... | collective-permute-start | bytes 393224 | tf_op jit(solution)/shard_map/ppermute | solution.py:30
  27.9 20.3 %collective-permute-start.3 = (bf16[64,1024]{1,0:T(8,128)(2,1)S(1)}, bf16[64,1024]{1,0:T(8,128)(2,1)S(1)}, u32[]{:S(2)}, u32[]{:S(2)}) collective-permute-start(bf16[64,1024]{1,0:T(8,128)(2,1)S(1)} %get-tuple-element.100), channel_id=1, source_target_pairs={{448,385},{449,386},{450,387},{451,388},{452,389},{453,390},{454,3... | collective-permute-start | bytes 393224 | tf_op jit(solution)/shard_map/ppermute | solution.py:30
  49.5 4.7 %collective-permute-start.11 = (bf16[512,256]{1,0:T(8,128)(2,1)S(1)}, bf16[512,256]{1,0:T(8,128)(2,1)S(1)}, u32[]{:S(2)}, u32[]{:S(2)}) collective-permute-start(bf16[512,256]{1,0:T(8,128)(2,1)S(1)} %get-tuple-element.123), channel_id=1, source_target_pairs={{0,1},{1,0},{2,3},{3,2},{4,5},{5,4},{6,7},{7,6},{8,9},{9,8},{10,11... | collective-permute-start | bytes 786440 | tf_op jit(solution)/shard_map/ppermute | solution.py:30
  52.1 3.3 %collective-permute-start.7 = (bf16[128,1024]{1,0:T(8,128)(2,1)S(1)}, bf16[128,1024]{1,0:T(8,128)(2,1)S(1)}, u32[]{:S(2)}, u32[]{:S(2)}) collective-permute-start(bf16[128,1024]{1,0:T(8,128)(2,1)S(1)} %get-tuple-element.115), channel_id=1, source_target_pairs={{384,320},{385,321},{386,322},{387,323},{388,324},{389,325},{390,3... | collective-permute-start | bytes 786440 | tf_op jit(solution)/shard_map/ppermute | solution.py:30
  54.7 3.3 %collective-permute-start.14 = (bf16[128,1024]{1,0:T(8,128)(2,1)S(1)}, bf16[128,1024]{1,0:T(8,128)(2,1)S(1)}, u32[]{:S(2)}, u32[]{:S(2)}) collective-permute-start(bf16[128,1024]{1,0:T(8,128)(2,1)S(1)} %get-tuple-element.130), channel_id=1, source_target_pairs={{320,256},{321,257},{322,258},{323,259},{324,260},{325,261},{326,2... | collective-permute-start | bytes 786440 | tf_op jit(solution)/shard_map/ppermute | solution.py:30
  62.5 3.5 %collective-permute-start.22 = (bf16[128,1024]{1,0:T(8,128)(2,1)S(1)}, bf16[128,1024]{1,0:T(8,128)(2,1)S(1)}, u32[]{:S(2)}, u32[]{:S(2)}) collective-permute-start(bf16[128,1024]{1,0:T(8,128)(2,1)S(1)} %get-tuple-element.146), channel_id=1, source_target_pairs={{192,128},{193,129},{194,130},{195,131},{196,132},{197,133},{198,1... | collective-permute-start | bytes 786440 | tf_op jit(solution)/shard_map/ppermute | solution.py:30
  63.9 3.9 %collective-permute-start.20 = (bf16[128,1024]{1,0:T(8,128)(2,1)S(1)}, bf16[128,1024]{1,0:T(8,128)(2,1)S(1)}, u32[]{:S(2)}, u32[]{:S(2)}) collective-permute-start(bf16[128,1024]{1,0:T(8,128)(2,1)S(1)} %get-tuple-element.144), channel_id=1, source_target_pairs={{192,128},{193,129},{194,130},{195,131},{196,132},{197,133},{198,1... | collective-permute-start | bytes 786440 | tf_op jit(solution)/shard_map/ppermute | solution.py:30
  66.6 75.5 %collective-permute-start.26 = (bf16[128,1024]{1,0:T(8,128)(2,1)S(1)}, bf16[128,1024]{1,0:T(8,128)(2,1)S(1)}, u32[]{:S(2)}, u32[]{:S(2)}) collective-permute-start(bf16[128,1024]{1,0:T(8,128)(2,1)S(1)} %get-tuple-element.154), channel_id=1, source_target_pairs={{128,64},{129,65},{130,66},{131,67},{132,68},{133,69},{134,70},{13... | collective-permute-start | bytes 786440 | tf_op jit(solution)/shard_map/ppermute | solution.py:30
  68.4 77.4 %collective-permute-start.24 = (bf16[128,1024]{1,0:T(8,128)(2,1)S(1)}, bf16[128,1024]{1,0:T(8,128)(2,1)S(1)}, u32[]{:S(2)}, u32[]{:S(2)}) collective-permute-start(bf16[128,1024]{1,0:T(8,128)(2,1)S(1)} %get-tuple-element.152), channel_id=1, source_target_pairs={{128,64},{129,65},{130,66},{131,67},{132,68},{133,69},{134,70},{13... | collective-permute-start | bytes 786440 | tf_op jit(solution)/shard_map/ppermute | solution.py:30
  69.7 72.3 %collective-permute-start.27 = (bf16[64,1024]{1,0:T(8,128)(2,1)S(1)}, bf16[64,1024]{1,0:T(8,128)(2,1)S(1)}, u32[]{:S(2)}, u32[]{:S(2)}) collective-permute-start(bf16[64,1024]{1,0:T(8,128)(2,1)S(1)} %get-tuple-element.155), channel_id=1, source_target_pairs={{128,127},{129,64},{130,65},{131,66},{132,67},{133,68},{134,69},{1... | collective-permute-start | bytes 393224 | tf_op jit(solution)/shard_map/ppermute | solution.py:30
  71.0 73.5 %collective-permute-start.25 = (bf16[64,1024]{1,0:T(8,128)(2,1)S(1)}, bf16[64,1024]{1,0:T(8,128)(2,1)S(1)}, u32[]{:S(2)}, u32[]{:S(2)}) collective-permute-start(bf16[64,1024]{1,0:T(8,128)(2,1)S(1)} %get-tuple-element.153), channel_id=1, source_target_pairs={{128,127},{129,64},{130,65},{131,66},{132,67},{133,68},{134,69},{1... | collective-permute-start | bytes 393224 | tf_op jit(solution)/shard_map/ppermute | solution.py:30
  143.2 9.0 %collective-permute-start.30 = (bf16[128,1024]{1,0:T(8,128)(2,1)S(1)}, bf16[128,1024]{1,0:T(8,128)(2,1)S(1)}, u32[]{:S(2)}, u32[]{:S(2)}) collective-permute-start(bf16[128,1024]{1,0:T(8,128)(2,1)S(1)} %get-tuple-element.162), channel_id=1, source_target_pairs={{64,0},{65,1},{66,2},{67,3},{68,4},{69,5},{70,6},{71,7},{72,8},{73... | collective-permute-start | bytes 786440 | tf_op jit(solution)/shard_map/ppermute | solution.py:30
  147.0 7.3 %collective-permute-start.28 = (bf16[128,1024]{1,0:T(8,128)(2,1)S(1)}, bf16[128,1024]{1,0:T(8,128)(2,1)S(1)}, u32[]{:S(2)}, u32[]{:S(2)}) collective-permute-start(bf16[128,1024]{1,0:T(8,128)(2,1)S(1)} %get-tuple-element.160), channel_id=1, source_target_pairs={{64,0},{65,1},{66,2},{67,3},{68,4},{69,5},{70,6},{71,7},{72,8},{73... | collective-permute-start | bytes 786440 | tf_op jit(solution)/shard_map/ppermute | solution.py:30
  148.3 3.9 %collective-permute-start.31 = (bf16[64,1024]{1,0:T(8,128)(2,1)S(1)}, bf16[64,1024]{1,0:T(8,128)(2,1)S(1)}, u32[]{:S(2)}, u32[]{:S(2)}) collective-permute-start(bf16[64,1024]{1,0:T(8,128)(2,1)S(1)} %get-tuple-element.163), channel_id=1, source_target_pairs={{64,1},{65,2},{66,3},{67,4},{68,5},{69,6},{70,7},{71,8},{72,9},{73... | collective-permute-start | bytes 393224 | tf_op jit(solution)/shard_map/ppermute | solution.py:30
  149.6 4.7 %collective-permute-start.29 = (bf16[64,1024]{1,0:T(8,128)(2,1)S(1)}, bf16[64,1024]{1,0:T(8,128)(2,1)S(1)}, u32[]{:S(2)}, u32[]{:S(2)}) collective-permute-start(bf16[64,1024]{1,0:T(8,128)(2,1)S(1)} %get-tuple-element.161), channel_id=1, source_target_pairs={{64,1},{65,2},{66,3},{67,4},{68,5},{69,6},{70,7},{71,8},{72,9},{73... | collective-permute-start | bytes 393224 | tf_op jit(solution)/shard_map/ppermute | solution.py:30
  154.8 11.3 %collective-permute-start.33 = (bf16[2,128,1024]{2,1,0:T(8,128)(2,1)S(1)}, bf16[2,128,1024]{2,1,0:T(8,128)(2,1)S(1)}, u32[]{:S(2)}, u32[]{:S(2)}) collective-permute-start(bf16[2,128,1024]{2,1,0:T(8,128)(2,1)S(1)} %shard_map.81.da), channel_id=1, source_target_pairs={{0,1},{1,0},{2,3},{3,2},{4,5},{5,4},{6,7},{7,6},{8,9},{9,8},{10,11... | collective-permute-start | bytes 1572872 | tf_op jit(solution)/shard_map/ppermute | solution.py:30
  189.0 30.5 %all-to-all-start = ((bf16[16,16,1024]{2,1,0:T(8,128)(2,1)}), bf16[16,16,1024]{2,1,0:T(8,128)(2,1)S(1)}, u32[]{:S(2)}, u32[]{:S(2)}) async-start(bf16[16,16,1024]{2,1,0:T(8,128)(2,1)} %copy-done.9), calls=%async_computation | async-start | bytes 1048576 | tf_op jit(solution)/shard_map/all_to_all | solution.py:369
  196.1 22.0 %collective-permute-start.32 = (bf16[2,32,1024]{2,1,0:T(8,128)(2,1)}, bf16[2,32,1024]{2,1,0:T(8,128)(2,1)S(1)}, u32[]{:S(2)}, u32[]{:S(2)}) collective-permute-start(bf16[2,32,1024]{2,1,0:T(8,128)(2,1)} %copy-done.10), channel_id=1, source_target_pairs={{64,65},{65,66},{66,67},{67,68},{68,69},{69,70},{70,71},{71,72},{7... | collective-permute-start | bytes 393224 | tf_op jit(solution)/shard_map/ppermute | solution.py:30
  209.1 13.9 %collective-permute-start.34 = (f32[16,1024]{1,0:T(8,128)}, f32[16,1024]{1,0:T(8,128)S(1)}, u32[]{:S(2)}, u32[]{:S(2)}) collective-permute-start(f32[16,1024]{1,0:T(8,128)} %shard_map.84), channel_id=1, source_target_pairs={{0,8},{1,9},{2,10},{3,11},{4,12},{5,13},{6,14},{7,15},{8,0},{9,1},... | collective-permute-start | bytes 196616 | tf_op jit(solution)/shard_map/ppermute | solution.py:30
  (23 other events, 269.8 us)
